TPU v7x, 32 devices: a whole 2x2x4 slice. The times are simulated.
32 devices in a mesh: day: 2 (over x), stn: 16 (over z, y, core).
Axes of the slice: x: 2, y: 2, z: 4, core: 2. Of those that a mesh axis runs over, the one named last changes fastest.
Arguments:
- station_partials: bfloat16 [131072, 128], P(('day', 'stn')), parts along dimension 0, may hold values from -6 to 6
- arc_partials: bfloat16 [131072, 128], P(('day', 'stn')), parts along dimension 0, may hold values from -6 to 6
- misclosure: bfloat16 [131072], P(('day', 'stn')), parts along dimension 0, may hold values from -6 to 6
- arc_id: int32 [131072, 1], P(('day', 'stn')), parts along dimension 0, may hold values from 0 to 31; in each aligned block of 4096 rows (0 to 4095, 4096 to 8191, ...) at most 256 rows name the same one
- arc_slot: int32 [64], P('day'), parts along dimension 0, may hold values from 0 to 31, each once
- arc_prior: float32 [64], P('day'), parts along dimension 0, may hold values from 0.1 to 1
Outputs:
- station_normal: float32 [32, 128, 128], P(('day', 'stn')), parts along dimension 0
- elimination: float32 [32, 128, 128], P(('day', 'stn')), parts along dimension 0
- elimination_rhs: float32 [32, 128], P(('day', 'stn')), parts along dimension 0
- arc_whitened: float32 [64, 128], P(('day', 'stn')), parts along dimension 0
There are 2 independent parts, one for each index of `day`. A program takes and returns all parts, laid end to end along the dimension named above; each array names one. Nothing has to cross between parts.
Inputs may be any that keep to these rules, and one draw needn't show every extreme that they name: `arc_id`: among the rows of one station no arc is named more than 256 times, and in every day some station names some arc exactly 256 times; every arc is seen by some station. `arc_slot`: each slot is given to exactly one arc.
All inputs are finite; a program needn't handle non-finite values.
Results may differ from a plain program's by a relative error of at most 0.0003.
Values may be sent and summed in bfloat16 or wider, within the bound.
No kernel may reach another device: no remote copies, remote signals or barrier semaphores. Data moves between devices by JAX's collectives and lax.ppermute only.
A program may use at most 128 MiB of HBM per device.

v0:
```python
import jax
import jax.numpy as jnp
from jax import lax
from jax.sharding import PartitionSpec as P


def bucket_rows(arc_ids, arc_slot, stn_rows, arc_rows, miss_rows, capacity):
    arc_count = arc_slot.shape[0]
    feature_width = stn_rows.shape[1]
    arc_table = jnp.arange(arc_count, dtype=jnp.int32)
    arc_match = (arc_ids[:, None] == arc_table[None, :]).astype(jnp.int32)
    slot_of_row = jnp.sum(arc_match * arc_slot[None, :], axis=1)
    onslot = (slot_of_row[:, None] == arc_table[None, :]).astype(jnp.int32)
    rank_in_slot = jnp.sum((jnp.cumsum(onslot, axis=0) - 1) * onslot, axis=1)
    positions = slot_of_row * capacity + rank_in_slot
    buffer_size = arc_count * capacity
    stn_buffer = jnp.zeros((buffer_size, feature_width), stn_rows.dtype).at[positions].set(stn_rows)
    arc_buffer = jnp.zeros((buffer_size, feature_width), arc_rows.dtype).at[positions].set(arc_rows)
    miss_buffer = jnp.zeros((buffer_size,), miss_rows.dtype).at[positions].set(miss_rows)
    return (stn_buffer, arc_buffer, miss_buffer)


def body(station_partials, arc_partials, misclosure, arc_id, arc_slot, arc_prior):
    groups = lax.axis_size("stn")
    arc_count = arc_slot.shape[0]
    per_dev = arc_count // groups
    row_count, feature_width = station_partials.shape
    capacity = 2 * row_count // arc_count
    station_normal = (
        jnp.einsum(
            "ri,rj->ij", station_partials, station_partials, preferred_element_type=jnp.float32
        )
        / row_count
    )[None]
    stn_buffer, arc_buffer, miss_buffer = bucket_rows(
        arc_id[:, 0], arc_slot, station_partials, arc_partials, misclosure, capacity
    )
    stn_buffer = stn_buffer.reshape(groups, per_dev, capacity, feature_width)
    arc_buffer = arc_buffer.reshape(groups, per_dev, capacity, feature_width)
    miss_buffer = miss_buffer.reshape(groups, per_dev, capacity)
    cross_part = jnp.einsum(
        "dkci,dkcj->kdji", stn_buffer, arc_buffer, preferred_element_type=jnp.float32
    )
    normal_part = jnp.einsum(
        "dkci,dkcj->kdij", arc_buffer, arc_buffer, preferred_element_type=jnp.float32
    )
    right_part = jnp.einsum(
        "dkci,dkc->kdi", arc_buffer, miss_buffer, preferred_element_type=jnp.float32
    )
    received = (
        lax.all_to_all(cross_part, "stn", split_axis=1, concat_axis=1, tiled=True),
        lax.all_to_all(normal_part, "stn", split_axis=1, concat_axis=1, tiled=True),
        lax.all_to_all(right_part, "stn", split_axis=1, concat_axis=1, tiled=True),
    )
    cross_tiles = received[0]
    arc_normal = jnp.sum(received[1], axis=1)
    arc_right = jnp.sum(received[2], axis=1)
    arc_table = jnp.arange(arc_count, dtype=jnp.int32)
    slot_match = (arc_slot[:, None] == arc_table[None, :]).astype(jnp.float32)
    prior_slot = jnp.sum(slot_match * arc_prior[:, None], axis=0)
    first_slot = lax.axis_index("stn") * per_dev
    prior_mine = lax.dynamic_slice_in_dim(prior_slot, first_slot, per_dev)
    identity = jnp.eye(feature_width, dtype=jnp.float32)
    factor = jnp.linalg.cholesky(arc_normal + (prior_mine * row_count)[:, None, None] * identity)
    arc_whitened = jax.scipy.linalg.solve_triangular(factor, arc_right[..., None], lower=True)[
        ..., 0
    ]
    stacked = jnp.transpose(cross_tiles, (0, 2, 1, 3)).reshape(
        per_dev, feature_width, groups * feature_width
    )
    solved = jax.scipy.linalg.solve_triangular(factor, stacked, lower=True)
    white_cross = jnp.transpose(
        solved.reshape(per_dev, feature_width, groups, feature_width), (0, 2, 1, 3)
    )
    schur_terms = jnp.einsum(
        "ksji,ksjl->sil", white_cross, white_cross, precision=lax.Precision.HIGHEST
    )
    rhs_terms = jnp.einsum(
        "ksji,kj->si", white_cross, arc_whitened, precision=lax.Precision.HIGHEST
    )
    schur_sum, rhs_sum = (
        lax.psum_scatter(schur_terms, "stn", scatter_dimension=0, tiled=True),
        lax.psum_scatter(rhs_terms, "stn", scatter_dimension=0, tiled=True),
    )
    elimination = schur_sum / feature_width
    elimination_rhs = rhs_sum / feature_width
    return (station_normal, elimination, elimination_rhs, arc_whitened)


def solution(mesh):
    in_specs = (
        P(("day", "stn"), None),
        P(("day", "stn"), None),
        P(("day", "stn")),
        P(("day", "stn"), None),
        P("day"),
        P("day"),
    )
    out_specs = (
        P(("day", "stn"), None, None),
        P(("day", "stn"), None, None),
        P(("day", "stn"), None),
        P(("day", "stn"), None),
    )
    return jax.shard_map(body, mesh=mesh, in_specs=in_specs, out_specs=out_specs, check_vma=False)
```

profile of v0, /device:TPU:0, one launch (start us, length us, event | category | flops | bytes accessed | tf_op | source)
XLA Modules:
  0.0 244.0 jit_solution(17787018640895750401)
XLA Ops:
  8.1 9.2 %reduce-window.6 = s32[32,32,128]{2,1,0:T(8,128)S(1)} reduce-window(s32[32,32,128]{2,1,0:T(8,128)S(1)} %fusion.19, s32[]{:T(128)} %constant.76.clone.1), window={size=1x1x128 pad=0_0x0_0x127_0}, to_apply=%region_1.0 | reduce-window | flops 16646144 | bytes 1048580 | tf_op jit(solution)/shard_map/reduce-window
  18.9 11.9 %scatter_custom_fusion = bf16[8192,128]{1,0:T(8,128)(2,1)S(1)} fusion(s32[4096]{0:T(1024)S(1)} %bitcast.92, bf16[4096,128]{1,0:T(8,128)(2,1)} %param.7, bf16[]{:T(256)} %constant.75.clone.1), kind=kCustom, calls=%fused_computation.15 | custom fusion | bytes 2097664 | tf_op jit(solution)/shard_map/scatter | solution.py:18
  30.8 2.1 fusion.30
  32.9 7.6 %all-to-all-start = ((f32[2,16,128,128]{3,2,0,1:T(8,128)}), f32[2,16,128,128]{3,2,0,1:T(8,128)}, u32[]{:S(2)}, u32[]{:S(2)}) async-start(f32[2,16,128,128]{3,2,0,1:T(8,128)} %fusion.30), calls=%async_computation | async-start | bytes 4194304 | tf_op jit(solution)/shard_map/all_to_all | solution.py:52
  40.5 12.5 %scatter_custom_fusion.1 = bf16[8192,128]{1,0:T(8,128)(2,1)} fusion(s32[4096]{0:T(1024)S(1)} %bitcast.93, bf16[4096,128]{1,0:T(8,128)(2,1)S(1)} %copy-done.2, bf16[]{:T(256)} %constant.75.clone.1), kind=kCustom, calls=%fused_computation.13 | custom fusion | bytes 2097154 | tf_op jit(solution)/shard_map/scatter | solution.py:17
  53.0 3.7 %fusion.31 = f32[2,16,128,128]{3,2,0,1:T(8,128)} fusion(bf16[16,2,256,128]{3,2,1,0:T(8,128)(2,1)S(1)} %bitcast.78, bf16[16,2,256,128]{3,2,1,0:T(8,128)(2,1)} %bitcast.82), kind=kOutput, calls=%fused_computation.54 | convolution fusion | flops 268435456 | bytes 6291456 | tf_op jit(solution)/shard_map/dkci,dkcj->kdji/dot_general | solution.py:41
  56.7 24.8 %all-to-all-done = f32[2,16,128,128]{3,2,0,1:T(8,128)} async-done(((f32[2,16,128,128]{3,2,0,1:T(8,128)}), f32[2,16,128,128]{3,2,0,1:T(8,128)}, u32[]{:S(2)}, u32[]{:S(2)}) %all-to-all-start) | async-done | bytes 2097184 | tf_op jit(solution)/shard_map/all_to_all | solution.py:52
  81.5 11.3 %all-to-all-start.1 = ((f32[2,16,128,128]{3,2,0,1:T(8,128)}), f32[2,16,128,128]{3,2,0,1:T(8,128)}, u32[]{:S(2)}, u32[]{:S(2)}) async-start(f32[2,16,128,128]{3,2,0,1:T(8,128)} %fusion.31), calls=%async_computation.1 | async-start | bytes 4194304 | tf_op jit(solution)/shard_map/all_to_all | solution.py:51
  94.4 1.7 reduce_sum.49
  96.2 1.4 add_multiply_fusion
  97.6 24.3 %custom-call.11 = f32[2,128,128]{2,1,0:T(8,128)S(1)} custom-call(f32[2,128,128]{2,1,0:T(8,128)} %add_multiply_fusion), custom_call_target="Cholesky" | custom-call | tf_op jit(solution)/shard_map/jit(cholesky)/cholesky | solution.py:64
  122.8 19.7 %custom-call.12 = f32[2,1,128,128]{2,3,1,0:T(8,128)S(1)} custom-call(f32[2,1,128,128]{3,2,1,0:T(8,128)S(1)} %select_bitcast_fusion), custom_call_target="InvertDiagBlocksLowerTriangular" | custom-call | tf_op jit(solution)/shard_map/jit(_solve_triangular)/vmap()/triangular_solve | solution.py:71
  142.5 3.0 %copy.44 = f32[2,16,128,128]{2,3,1,0:T(8,128)} copy(f32[2,16,128,128]{3,2,0,1:T(8,128)} %all-to-all-done.1) | data formatting | bytes 4194304 | tf_op jit(solution)/shard_map/all_to_all | solution.py:51
  145.5 3.5 %fusion.22 = f32[2,128,2048]{2,1,0:T(8,128)S(1)} fusion(f32[2,128,2048]{1,2,0:T(8,128)} %bitcast.83, f32[2,1,128,128]{2,3,1,0:T(8,128)S(1)} %custom-call.12), kind=kOutput, calls=%fused_computation.29 | convolution fusion | flops 805306368 | bytes 4325376 | tf_op jit(solution)/shard_map/jit(_solve_triangular)/vmap()/triangular_solve | solution.py:71
  149.0 1.7 copy.68
  150.7 3.0 %copy.47 = f32[2,128,16,128]{1,3,0,2:T(8,128)} copy(f32[2,128,16,128]{3,2,1,0:T(8,128)} %bitcast.80) | data formatting | bytes 4194304 | tf_op jit(solution)/shard_map/reshape | solution.py:73
  153.7 1.9 bitcast_bitcast_fusion.1
  155.9 3.6 %fusion.7 = f32[16,128,128]{2,1,0:T(8,128)} fusion(f32[2,16,128,128]{3,1,2,0:T(8,128)S(1)} %bitcast_bitcast_fusion.1, f32[2,128,16,128]{1,3,0,2:T(8,128)S(1)} %copy-done), kind=kOutput, calls=%fused_computation.10 | convolution fusion | flops 805306368 | bytes 5242880 | tf_op jit(solution)/shard_map/ksji,ksjl->sil/dot_general | solution.py:75
  159.6 28.7 %scatter_custom_fusion.2 = bf16[8192]{0:T(1024)(128)(2,1)S(1)} fusion(s32[4096]{0:T(1024)} %bitcast.94, bf16[4096]{0:T(1024)(128)(2,1)} %param.8, bf16[]{:T(256)} %constant.75.clone.1), kind=kCustom, calls=%fused_computation.46 | custom fusion | bytes 16896 | tf_op jit(solution)/shard_map/scatter | solution.py:19
  189.3 6.1 %all-to-all-start.2 = ((f32[2,16,128]{2,0,1:T(2,128)}), f32[2,16,128]{2,0,1:T(2,128)S(1)}, u32[]{:S(2)}, u32[]{:S(2)}) async-start(f32[2,16,128]{2,0,1:T(2,128)} %bitcast.74), calls=%async_computation.3 | async-start | bytes 32768 | tf_op jit(solution)/shard_map/all_to_all | solution.py:53
  197.1 4.9 %all-to-all-done.2 = f32[2,16,128]{2,0,1:T(2,128)S(1)} async-done(((f32[2,16,128]{2,0,1:T(2,128)}), f32[2,16,128]{2,0,1:T(2,128)S(1)}, u32[]{:S(2)}, u32[]{:S(2)}) %all-to-all-start.2) | async-done | bytes 16416 | tf_op jit(solution)/shard_map/all_to_all | solution.py:53
  202.2 1.9 fusion.2
  204.1 30.5 %all-reduce = f32[16,128]{1,0:T(8,128)S(1)} all-reduce(f32[16,128]{1,0:T(8,128)S(1)} %bitcast.90), channel_id=3, replica_groups=mesh['day'=2,'stn'=16] {'stn'}, use_global_device_ids=true, to_apply=%region_13.14.clone | all-reduce | flops 2048 | bytes 16384
  235.7 1.5 broadcast_multiply_fusion
  (45 shorter events, 9.5 us)
Async XLA Ops:
  18.9 21.6 %copy-start.3 = (s32[4096,1]{0,1:T(1,128)}, s32[4096,1]{0,1:T(1,128)S(1)}, u32[]{:S(2)}) copy-start(s32[4096,1]{0,1:T(1,128)S(1)} %compare_select_fusion) | copy-start | bytes 49156
  32.9 7.6 %copy-start.2 = (bf16[4096,128]{1,0:T(8,128)(2,1)S(1)}, bf16[4096,128]{1,0:T(8,128)(2,1)}, u32[]{:S(2)}) copy-start(bf16[4096,128]{1,0:T(8,128)(2,1)} %param.6) | copy-start | bytes 3145732
  32.9 48.6 %all-to-all-start = ((f32[2,16,128,128]{3,2,0,1:T(8,128)}), f32[2,16,128,128]{3,2,0,1:T(8,128)}, u32[]{:S(2)}, u32[]{:S(2)}) async-start(f32[2,16,128,128]{3,2,0,1:T(8,128)} %fusion.30), calls=%async_computation | async-start | bytes 4194304 | tf_op jit(solution)/shard_map/all_to_all | solution.py:52
  56.7 36.3 %copy-start.5 = (s32[32]{0:T(128)S(1)}, s32[32]{0:T(128)}, u32[]{:S(2)}) copy-start(s32[32]{0:T(128)} %param.10) | copy-start | bytes 388
  56.7 36.4 %copy-start.6 = (f32[32]{0:T(128)S(1)}, f32[32]{0:T(128)}, u32[]{:S(2)}) copy-start(f32[32]{0:T(128)} %param.11) | copy-start | bytes 388
  81.5 61.0 %all-to-all-start.1 = ((f32[2,16,128,128]{3,2,0,1:T(8,128)}), f32[2,16,128,128]{3,2,0,1:T(8,128)}, u32[]{:S(2)}, u32[]{:S(2)}) async-start(f32[2,16,128,128]{3,2,0,1:T(8,128)} %fusion.31), calls=%async_computation.1 | async-start | bytes 4194304 | tf_op jit(solution)/shard_map/all_to_all | solution.py:51
  92.8 142.9 %reduce-scatter.2.cloned.1.call-start = ((), (), s32[]{:S(2)}) async-start(), calls=%async_computation.4 | async-start | bytes 1114112 | tf_op jit(solution)/shard_map/reduce_scatter | solution.py:82
  153.7 2.2 copy-start
  188.3 8.2 %copy-start.7 = (u32[32]{0:T(128)S(1)}, u32[32]{0:T(128)}, u32[]{:S(2)}) copy-start(u32[32]{0:T(128)} %constant.91) | copy-start | bytes 388
  188.7 13.5 %copy-start.1 = (f32[2,128,16,128]{1,3,0,2:T(8,128)S(1)}, f32[2,128,16,128]{1,3,0,2:T(8,128)}, u32[]{:S(2)}) copy-start(f32[2,128,16,128]{1,3,0,2:T(8,128)} %copy.47) | copy-start | bytes 6291460
  189.3 12.6 %all-to-all-start.2 = ((f32[2,16,128]{2,0,1:T(2,128)}), f32[2,16,128]{2,0,1:T(2,128)S(1)}, u32[]{:S(2)}, u32[]{:S(2)}) async-start(f32[2,16,128]{2,0,1:T(2,128)} %bitcast.74), calls=%async_computation.3 | async-start | bytes 32768 | tf_op jit(solution)/shard_map/all_to_all | solution.py:53
  202.2 35.0 %copy-start.4 = (f32[2,1,128]{2,1,0:T(1,128)}, f32[2,1,128]{2,1,0:T(1,128)S(1)}, u32[]{:S(2)}) copy-start(f32[2,1,128]{2,1,0:T(1,128)S(1)} %fusion.20) | copy-start | bytes 3076
Sparse Core Ops, SparseCore 0:
  159.7 58.9 reduce-scatter.1
where the time goes:
time: 245 us; the launch traced here: 244 us
  local copies, waits for them, and re-layouts  65 us (27%)
  other arithmetic  62.8 us (26%)
  blocking collectives  30.5 us (12%)
  waiting for transfers between devices  29.7 us (12%)
  starting transfers between devices  25.2 us (10%)
  matrix products  16.5 us (7%)
  between operations  14.3 us (6%)
    unnamed x1, blocking collectives  30.5 us
    scatter x1, local copies, waits for them, and re-layouts, bucket_rows(): jnp.zeros((buffer_size,), miss_rows.dtype).at[positions].set(miss_rows)  28.7 us
    another operation x4, other arithmetic, body(): jnp.linalg.cholesky(arc_normal + (prior_mine * row_count)[:, None, None]...  25.8 us
    all_to_all x1, waiting for transfers between devices, body(): lax.all_to_all(normal_part, 'stn', split_axis=1, concat_axis=1, tiled=True)  24.8 us
    another operation x3, other arithmetic, body(): solved = jax.scipy.linalg.solve_triangular(factor, stacked, lower=True)  19.8 us
    scatter x1, local copies, waits for them, and re-layouts, bucket_rows(): jnp.zeros((buffer_size, feature_width), stn_rows.dtype).at[positions]  12.5 us
    scatter x1, local copies, waits for them, and re-layouts, bucket_rows(): jnp.zeros((buffer_size, feature_width), arc_rows.dtype).at[positions]  11.9 us
    all_to_all x1, starting transfers between devices, body(): lax.all_to_all(cross_part, 'stn', split_axis=1, concat_axis=1, tiled=True)  11.3 us
  transfers between devices with their start and end apart: 4, of which 2 were waited for; matrix products, arithmetic and copies ran while one was open for 41% of the time, Pallas kernels for 0%

commit v1 on v0

v1 whole, which is shorter than its diff:
```python
import functools

import jax
import jax.numpy as jnp
from jax import lax
from jax.experimental import pallas as pl
from jax.experimental.pallas import tpu as pltpu
from jax.sharding import PartitionSpec as P


EXTRA = 8
LIMITED = pltpu.CompilerParams(vmem_limit_bytes=24 * 2**20)
NT = (((1,), (1,)), ((), ()))
NN = (((1,), (0,)), ((), ()))


def split(value):
    high = value.astype(jnp.bfloat16)
    return high, (value - high.astype(jnp.float32)).astype(jnp.bfloat16)


def arcs_of_slots(slot_ref, arc_ref, arcs):
    def put(arc, _):
        arc_ref[slot_ref[arc]] = arc
        return 0

    lax.fori_loop(0, arcs, put, 0)


def tiles_kernel(owners, want_table, want_own, *refs):
    slot_ref, id_ref, miss_ref, stn_rows_ref, arc_rows_ref = refs[:5]
    table_ref, sent_ref, kept_ref, cross_ref = refs[5:9]
    own_ref = refs[9] if want_own else None
    arc_ref, ids_sc = refs[-2:]
    rows, width = arc_rows_ref.shape
    arcs = slot_ref.shape[0]
    me = lax.axis_index("stn")
    arcs_of_slots(slot_ref, arc_ref, arcs)
    ids_sc[...] = jnp.broadcast_to(id_ref[...].astype(jnp.float32), ids_sc.shape)
    if want_table:
        table_ref[...] = arc_rows_ref[...].T
    mine = []
    for owner in owners:
        first = 2 * jnp.bitwise_xor(me, owner)
        mine += [arc_ref[first], arc_ref[first + 1]]
    sub16 = lax.broadcasted_iota(jnp.int32, ids_sc.shape, 0)
    named = jnp.full(ids_sc.shape, -1.0, jnp.float32)
    left = []
    for at, arc in enumerate(mine):
        arc = arc.astype(jnp.float32)
        hit = jnp.where(ids_sc[...] == arc, 1.0, 0.0).astype(jnp.bfloat16)
        table = table_ref[...].reshape(width // 16, 16, rows)
        left.append((table * hit[None]).reshape(width, rows))
        named = jnp.where(sub16 == at, arc, named)
    hit = jnp.where(ids_sc[...] == named, 1.0, 0.0).astype(jnp.bfloat16)
    miss = miss_ref[...].astype(jnp.float32)
    miss = jnp.concatenate([miss[at : at + 1] for at in range(miss.shape[0])], axis=1)
    left.append(hit * jnp.broadcast_to(miss, hit.shape).astype(jnp.bfloat16))
    right = jnp.concatenate([arc_rows_ref[...], stn_rows_ref[...]], axis=1)
    full = lax.dot_general(
        jnp.concatenate(left, axis=0), right, NN, preferred_element_type=jnp.float32
    )
    r = lax.broadcasted_iota(jnp.int32, (width, width), 0)
    c = lax.broadcasted_iota(jnp.int32, (width, width), 1)
    sub = lax.broadcasted_iota(jnp.int32, (EXTRA, width), 0)
    rights = full[len(mine) * width :, :width]
    half = len(owners) // 2
    for at in range(len(owners)):
        top = 2 * at * width
        first, second = full[top : top + width, :width], full[top + width : top + 2 * width, :width]
        out_ref = sent_ref if at < half else kept_ref
        out_ref[at % half, 0:width, :] = jnp.where(r >= c, first, second)
        diag = jnp.sum(jnp.where(r == c, second, 0.0), axis=0, keepdims=True)
        tail = jnp.where(sub == 0, diag, 0.0)
        tail = jnp.where(sub == 1, rights[2 * at : 2 * at + 1], tail)
        out_ref[at % half, width:, :] = jnp.where(sub == 2, rights[2 * at + 1 : 2 * at + 2], tail)
        for side in range(2):
            cross = full[top + side * width : top + (side + 1) * width, width:]
            cross_ref[2 * at + side, :, :width], cross_ref[2 * at + side, :, width:] = split(cross)
    if want_own:
        own = lax.dot_general(
            stn_rows_ref[...].T, stn_rows_ref[...], NN, preferred_element_type=jnp.float32
        )
        own_ref[0] = own / rows


def lanes_of(block, k):
    return jnp.broadcast_to(block[:, k : k + 1], block.shape)


def rows_of(block, k):
    return jnp.broadcast_to(block[k : k + 1, :], block.shape)


def inverse_root(value):
    guess = lax.rsqrt(value)
    return guess * (1.5 - 0.5 * value * guess * guess)


def eliminate_panel(tile, panel, sub, lane):
    base = 8 * panel
    inside = (lane >= base) & (lane < base + 8)
    top = tile[panel]
    columns = [lanes_of(top, base + j) for j in range(8)]
    low = {(i, j): rows_of(columns[j], i) for j in range(8) for i in range(j, 8)}
    start = jnp.where(inside, jnp.where(lane - base == sub, 1.0, 0.0), top)
    white = [rows_of(start, i) for i in range(8)]
    root = []
    for j in range(8):
        root.append(inverse_root(low[j, j]))
        for i in range(j + 1, 8):
            low[i, j] = low[i, j] * root[j]
        for k in range(j + 1, 8):
            for i in range(k, 8):
                low[i, k] = low[i, k] - low[i, j] * low[k, j]
        white[j] = white[j] * root[j]
        for i in range(j + 1, 8):
            white[i] = white[i] - low[i, j] * white[j]
    done = white[0]
    for j in range(1, 8):
        done = jnp.where(sub == j, white[j], done)
    tile[panel] = done
    if panel + 1 == len(tile):
        return
    back = list(white)
    for j in reversed(range(8)):
        back[j] = back[j] * root[j]
        for i in range(j):
            back[i] = back[i] - low[j, i] * back[j]
    for t in range(panel + 1, len(tile)):
        rest = jnp.where(inside, 0.0, tile[t])
        for j in reversed(range(8)):
            rest = rest - lanes_of(tile[t], base + j) * back[j]
        tile[t] = rest


def factor_kernel(rows, slot_ref, prior_ref, *refs):
    (out_ref, sys_sc), terms = refs[-2:], refs[:-2]
    width = out_ref.shape[-1]
    arcs = slot_ref.shape[0]
    me = lax.axis_index("stn")

    def find(arc, found):
        hit = slot_ref[arc]
        weight = prior_ref[arc]
        return (
            jnp.where(hit == 2 * me, weight, found[0]),
            jnp.where(hit == 2 * me + 1, weight, found[1]),
        )

    priors = lax.fori_loop(0, arcs, find, (jnp.float32(0), jnp.float32(0)))
    whole = sum([term[0] for term in terms[1:]], terms[0][0])
    packed, tail = whole[:width], whole[width:]
    flipped = packed.T
    r = lax.broadcasted_iota(jnp.int32, (width, width), 0)
    c = lax.broadcasted_iota(jnp.int32, (width, width), 1)
    eye = r == c
    first = jnp.where(r >= c, packed, flipped)
    second = jnp.where(r < c, packed, flipped)
    second = jnp.where(eye, tail[0:1, :], second)
    sys_sc[0] = first + jnp.where(eye, priors[0] * rows, 0.0)
    sys_sc[1] = second + jnp.where(eye, priors[1] * rows, 0.0)
    tiles = width // 8
    sub = lax.broadcasted_iota(jnp.int32, (8, width), 0)
    lane = lax.broadcasted_iota(jnp.int32, (8, width), 1)
    state = [[sys_sc[m, 8 * t : 8 * t + 8, :] for t in range(tiles)] for m in range(2)]
    for panel in range(tiles):
        for m in range(2):
            eliminate_panel(state[m], panel, sub, lane)
    for m in range(2):
        for t in range(tiles):
            sys_sc[m, 8 * t : 8 * t + 8, :] = state[m][t]
    inverses = [jnp.where(r >= c, sys_sc[m], 0.0) for m in range(2)]
    whitened = [
        lax.dot_general(
            tail, inverses[m], NT, precision=lax.Precision.HIGHEST, preferred_element_type=jnp.float32
        )[m + 1 : m + 2]
        for m in range(2)
    ]
    out_ref[0, 0:width, :] = jnp.where(r >= c, inverses[0], inverses[1].T)
    diag = jnp.sum(jnp.where(eye, inverses[1], 0.0), axis=0, keepdims=True)
    last = jnp.where(sub == 0, diag, 0.0)
    last = jnp.where(sub == 1, whitened[0], last)
    out_ref[0, width:, :] = jnp.where(sub == 2, whitened[1], last)


def eliminate_kernel(places, *refs):
    pieces, refs = refs[: len(places)], refs[len(places) :]
    crosses, (elim_ref, rhs_ref, sum_sc) = refs[:-3], refs[-3:]
    width = elim_ref.shape[1]
    r = lax.broadcasted_iota(jnp.int32, (width, width), 0)
    c = lax.broadcasted_iota(jnp.int32, (width, width), 1)
    rows16 = lax.broadcasted_iota(jnp.int32, (16, 2 * width), 0)
    for count, (piece_ref, (chunk, at)) in enumerate(zip(pieces, places)):
        packed = piece_ref[0, 0:width, :]
        tail = piece_ref[0, width:, :]
        second = jnp.where(r < c, packed, jnp.where(r == c, tail[0:1, :], 0.0)).T
        first = jnp.where(r >= c, packed, 0.0)
        highs, lows = [], []
        for side, factor in enumerate((first, second)):
            left = jnp.concatenate(split(factor), axis=1)
            cross = crosses[chunk][2 * at + side]
            kept = jnp.concatenate([cross[:, :width], jnp.zeros((width, width), cross.dtype)], axis=1)
            both = lax.dot_general(
                left, jnp.concatenate([cross, kept], axis=0), NN, preferred_element_type=jnp.float32
            )
            high, low = split(both[:, :width] + both[:, width:])
            highs.append(high)
            lows.append(low)
        white_high, white_low = jnp.concatenate(highs, axis=0), jnp.concatenate(lows, axis=0)
        right = jnp.concatenate([white_high, white_low], axis=1)
        w_high, w_low = split(jnp.concatenate([tail[1:2], tail[2:3]], axis=1))
        w_rows = jnp.where(
            rows16 == 0,
            w_high.astype(jnp.float32),
            jnp.where(rows16 == 1, w_low.astype(jnp.float32), 0.0),
        ).astype(jnp.bfloat16)
        left = jnp.concatenate([white_high.T, w_rows], axis=0)
        term = lax.dot_general(left, right, NN, preferred_element_type=jnp.float32)
        if count:
            sum_sc[...] += term
        else:
            sum_sc[...] = term
    total = sum_sc[...]
    mixed = total[:width, width:]
    elim_ref[0] = (total[:width, :width] + (mixed + mixed.T)) / width
    w_part = total[width : width + 8]
    rhs_ref[...] = (w_part[0:1, :width] + w_part[0:1, width:] + w_part[1:2, :width]) / width


def body(station_partials, arc_partials, misclosure, arc_id, arc_slot, arc_prior):
    groups = lax.axis_size("stn")
    bits = groups.bit_length() - 1
    arcs = arc_slot.shape[0]
    rows, width = station_partials.shape
    ids = arc_id.reshape(1, rows)
    miss = misclosure.reshape(rows // width, width)
    smem = pl.BlockSpec(memory_space=pltpu.SMEM)
    vmem = pl.BlockSpec(memory_space=pltpu.VMEM)
    f32, bf16 = jnp.float32, jnp.bfloat16
    tall = width + EXTRA

    def swap(value, flip):
        return lax.ppermute(value, "stn", [(at, at ^ flip) for at in range(groups)])

    chunks = groups // 4
    crosses, where, terms = [], {}, []
    for chunk in range(chunks):
        far = groups - 4 * (chunk + 1)
        owners = [far + 1, far + 3, far, far + 2]
        want_own = chunk == chunks - 1
        shapes = [
            jax.ShapeDtypeStruct((2, tall, width), f32),
            jax.ShapeDtypeStruct((2, tall, width), f32),
            jax.ShapeDtypeStruct((2 * len(owners), width, 2 * width), bf16),
        ]
        if chunk == 0:
            shapes.insert(0, jax.ShapeDtypeStruct((width, rows), bf16))
        if want_own:
            shapes.append(jax.ShapeDtypeStruct((1, width, width), f32))
        operands = [arc_slot, ids, miss, station_partials, arc_partials]
        if chunk:
            operands.append(table)
        found = pl.pallas_call(
            functools.partial(tiles_kernel, tuple(owners), chunk == 0, want_own),
            out_shape=shapes,
            in_specs=[smem] + [vmem] * (len(operands) - 1),
            out_specs=[vmem] * len(shapes),
            scratch_shapes=[pltpu.SMEM((arcs,), jnp.int32), pltpu.VMEM((16, rows), f32)],
            cost_estimate=pl.CostEstimate(
                flops=2 * rows * 2 * len(owners) * width * 2 * width,
                bytes_accessed=4 * rows * width,
                transcendentals=0,
            ),
            compiler_params=LIMITED,
            name="tiles",
        )(*operands)
        if chunk == 0:
            table, found = found[0], found[1:]
        sent, kept, cross, *own = found
        crosses.append(cross)
        where.update({owner: (chunk, at) for at, owner in enumerate(owners)})
        came = swap(sent, 1)
        for at, owner in enumerate(owners[2:]):
            if owner:
                both = kept[at : at + 1] + came[at : at + 1]
                terms.append(swap(both, owner))
            else:
                terms += [kept[at : at + 1], came[at : at + 1]]
    (station_normal,) = own
    mine = pl.pallas_call(
        functools.partial(factor_kernel, float(rows)),
        out_shape=jax.ShapeDtypeStruct((1, tall, width), f32),
        in_specs=[smem, smem] + [vmem] * len(terms),
        out_specs=vmem,
        scratch_shapes=[pltpu.VMEM((2, width, width), f32)],
        compiler_params=LIMITED,
        name="factor",
    )(arc_slot, arc_prior, *terms)
    arc_whitened = mine[0, width + 1 : width + 3, :]
    pieces = {0: mine}
    for bit in reversed(range(bits)):
        pieces.update({owner ^ (1 << bit): swap(piece, 1 << bit) for owner, piece in pieces.items()})
    elimination, elimination_rhs = pl.pallas_call(
        functools.partial(eliminate_kernel, tuple(where[owner] for owner in pieces)),
        out_shape=[
            jax.ShapeDtypeStruct((1, width, width), f32),
            jax.ShapeDtypeStruct((1, width), f32),
        ],
        in_specs=[vmem] * (len(pieces) + chunks),
        out_specs=[vmem, vmem],
        scratch_shapes=[pltpu.VMEM((width + 16, 2 * width), f32)],
        compiler_params=LIMITED,
        name="eliminate",
    )(*pieces.values(), *crosses)
    return (station_normal, elimination, elimination_rhs, arc_whitened)


def solution(mesh):
    in_specs = (
        P(("day", "stn"), None),
        P(("day", "stn"), None),
        P(("day", "stn")),
        P(("day", "stn"), None),
        P("day"),
        P("day"),
    )
    out_specs = (
        P(("day", "stn"), None, None),
        P(("day", "stn"), None, None),
        P(("day", "stn"), None),
        P(("day", "stn"), None),
    )
    return jax.shard_map(body, mesh=mesh, in_specs=in_specs, out_specs=out_specs, check_vma=False)
```

time: 245 us -> 66.8 us (0.27)
  other arithmetic: 62.8 us -> 0.07 us
  local copies, waits for them, and re-layouts: 65 us -> 5.73 us
  blocking collectives: 30.5 us -> 0 us
  Pallas kernels: 0 us -> 25 us
  matrix products: 16.5 us -> 0 us
  waiting for transfers between devices: 29.7 us -> 13.4 us
  between operations: 14.3 us -> 0.76 us
  starting transfers between devices: 25.2 us -> 21.5 us
    another operation x9 -> x0, other arithmetic: 55 us -> none  [the longest x4 25.8 us: body(): jnp.linalg.cholesky(arc_normal + (prior_mine * row_count)[:, None, None]...]
    scatter x3 -> x0, local copies, waits for them, and re-layouts: 53.1 us -> none  [the longest x1 28.7 us: bucket_rows(): jnp.zeros((buffer_size,), miss_rows.dtype).at[positions].set(miss_rows)]
    unnamed x1 -> x0, blocking collectives: 30.5 us -> none
    all_to_all x3 -> x0, waiting for transfers between devices: 29.7 us -> none  [the longest x1 24.8 us: body(): lax.all_to_all(normal_part, 'stn', split_axis=1, concat_axis=1, tiled=True)]
    pallas_call x0 -> x6, Pallas kernels: none -> 25 us  [the longest x4 13.9 us: body(): pl.pallas_call(functools.partial(tiles_kernel, tuple(owners), chunk == 0,...]
    all_to_all x3 -> x0, starting transfers between devices: 24.9 us -> none  [the longest x1 11.3 us: body(): lax.all_to_all(cross_part, 'stn', split_axis=1, concat_axis=1, tiled=True)]
    ppermute x0 -> x26, starting transfers between devices: none -> 21.5 us  [swap(): return lax.ppermute(value, 'stn', [(at, at ^ flip) for at in range(groups)])]
    ppermute x0 -> x26, waiting for transfers between devices: none -> 13.4 us  [swap(): return lax.ppermute(value, 'stn', [(at, at ^ flip) for at in range(groups)])]
  transfers between devices with their start and end apart: 4 -> 26, of which waited for: 2 -> 11; matrix products, arithmetic and copies ran while one was open for 41% -> 1% of each run, Pallas kernels for 0% -> 16%
where the time goes in v1:
time: 66.8 us; the launch traced here: 66.4 us
  Pallas kernels  25 us (37%)
  starting transfers between devices  21.5 us (32%)
  waiting for transfers between devices  13.4 us (20%)
  local copies, waits for them, and re-layouts  5.73 us (9%)
  between operations  0.76 us (1%)
    ppermute x26, starting transfers between devices, swap(): return lax.ppermute(value, 'stn', [(at, at ^ flip) for at in range(groups)])  21.5 us
    pallas_call x4, Pallas kernels, body(): pl.pallas_call(functools.partial(tiles_kernel, tuple(owners), chunk == 0,...  13.9 us
    ppermute x26, waiting for transfers between devices, swap(): return lax.ppermute(value, 'stn', [(at, at ^ flip) for at in range(groups)])  13.4 us
    pallas_call x1, Pallas kernels, body(): pl.pallas_call(functools.partial(factor_kernel, float(rows)), out_shape=j...  7.93 us
    unnamed x12, local copies, waits for them, and re-layouts  5.17 us
    pallas_call x1, Pallas kernels, body(): pl.pallas_call(functools.partial(eliminate_kernel, tuple((where[owner] fo...  3.2 us
  transfers between devices with their start and end apart: 26, of which 11 were waited for; matrix products, arithmetic and copies ran while one was open for 1% of the time, Pallas kernels for 16%

profile of v1, /device:TPU:0, one launch (start us, length us, event | category | flops | bytes accessed | tf_op | source)
XLA Modules:
  0.0 66.4 jit_solution(13824160810988817971)
XLA Ops:
  1.3 1.2 %copy-done.2 = bf16[4096,128]{1,0:T(8,128)(2,1)S(1)} copy-done((bf16[4096,128]{1,0:T(8,128)(2,1)S(1)}, bf16[4096,128]{1,0:T(8,128)(2,1)}, u32[]{:S(2)}) %copy-start.2) | copy-done | bytes 1048600
  2.5 1.2 %copy-done.3 = bf16[4096,128]{1,0:T(8,128)(2,1)S(1)} copy-done((bf16[4096,128]{1,0:T(8,128)(2,1)S(1)}, bf16[4096,128]{1,0:T(8,128)(2,1)}, u32[]{:S(2)}) %copy-start.3) | copy-done | bytes 1048600
  3.7 0.7 %copy-done.4 = s32[4096,1]{0,1:T(1,128)S(1)} copy-done((s32[4096,1]{0,1:T(1,128)S(1)}, s32[4096,1]{0,1:T(1,128)}, u32[]{:S(2)}) %copy-start.4) | copy-done | bytes 16408
  5.2 3.3 %tiles.4 = (bf16[128,4096]{1,0:T(8,128)(2,1)S(1)}, f32[2,136,128]{2,1,0:T(8,128)S(1)}, f32[2,136,128]{2,1,0:T(8,128)S(1)}, bf16[8,128,256]{2,1,0:T(8,128)(2,1)S(1)}) custom-call(s32[32]{0:T(128)S(1)} %copy-done, s32[1,4096]{1,0:T(1,128)S(1)} %bitcast.4, bf16[32,128]{1,0:T(8,128)(2,1)S(1)} %bitcast.8, bf16[4096,128]{1,0:T(8,128)(2,1)S(1)} %copy-done.2, ...), custom_call_target="tpu_custom_call" | custom-call | flops 2147483648 | bytes 2097152 | tf_op jit(solution)/shard_map/tiles/pallas_call | solution.py:264
  9.0 3.2 %tiles.7 = (f32[2,136,128]{2,1,0:T(8,128)S(1)}, f32[2,136,128]{2,1,0:T(8,128)S(1)}, bf16[8,128,256]{2,1,0:T(8,128)(2,1)S(1)}) custom-call(s32[32]{0:T(128)S(1)} %copy-done, s32[1,4096]{1,0:T(1,128)S(1)} %bitcast.5, bf16[32,128]{1,0:T(8,128)(2,1)S(1)} %bitcast.9, bf16[4096,128]{1,0:T(8,128)(2,1)S(1)} %copy-done.2, bf16[4096,128]{1,0:T(8,128)(2,1)S(1)} %copy-done.3, ...), custom_call_target="tpu_custom_call" | custom-call | flops 2147483648 | bytes 2097152 | tf_op jit(solution)/shard_map/tiles/pallas_call | solution.py:264
  12.3 3.2 %tiles.6 = (f32[2,136,128]{2,1,0:T(8,128)S(1)}, f32[2,136,128]{2,1,0:T(8,128)S(1)}, bf16[8,128,256]{2,1,0:T(8,128)(2,1)S(1)}) custom-call(s32[32]{0:T(128)S(1)} %copy-done, s32[1,4096]{1,0:T(1,128)S(1)} %bitcast.6, bf16[32,128]{1,0:T(8,128)(2,1)S(1)} %bitcast.10, bf16[4096,128]{1,0:T(8,128)(2,1)S(1)} %copy-done.2, bf16[4096,128]{1,0:T(8,128)(2,1)S(1)} %copy-done.3, ...), custom_call_target="tpu_custom_call" | custom-call | flops 2147483648 | bytes 2097152 | tf_op jit(solution)/shard_map/tiles/pallas_call | solution.py:264
  16.1 4.1 %tiles.5 = (f32[2,136,128]{2,1,0:T(8,128)S(1)}, f32[2,136,128]{2,1,0:T(8,128)S(1)}, bf16[8,128,256]{2,1,0:T(8,128)(2,1)S(1)}, f32[1,128,128]{2,1,0:T(8,128)}) custom-call(s32[32]{0:T(128)S(1)} %copy-done, s32[1,4096]{1,0:T(1,128)S(1)} %bitcast.7, bf16[32,128]{1,0:T(8,128)(2,1)S(1)} %bitcast.11, bf16[4096,128]{1,0:T(8,128)(2,1)S(1)} %copy-done.2, ...), custom_call_target="tpu_custom_call" | custom-call | flops 2147483648 | bytes 2097152 | tf_op jit(solution)/shard_map/tiles/pallas_call | solution.py:264
  20.3 6.1 %collective-permute-start.2 = (f32[1,136,128]{2,1,0:T(8,128)S(1)}, f32[1,136,128]{2,1,0:T(8,128)S(1)}, u32[]{:S(2)}, u32[]{:S(2)}) collective-permute-start(f32[1,136,128]{2,1,0:T(8,128)S(1)} %get-tuple-element.40), channel_id=1, source_target_pairs={{0,14},{1,15},{2,12},{3,13},{4,10},{5,11},{6,8},{7,9},{8,6},{9,7},... | collective-permute-start | bytes 208904 | tf_op jit(solution)/shard_map/ppermute | solution.py:244
  26.7 1.9 %collective-permute-start.7 = (f32[1,136,128]{2,1,0:T(8,128)S(1)}, f32[1,136,128]{2,1,0:T(8,128)S(1)}, u32[]{:S(2)}, u32[]{:S(2)}) collective-permute-start(f32[1,136,128]{2,1,0:T(8,128)S(1)} %get-tuple-element.37), channel_id=1, source_target_pairs={{0,4},{1,5},{2,6},{3,7},{4,0},{5,1},{6,2},{7,3},{8,12},{9,13},{10,... | collective-permute-start | bytes 208904 | tf_op jit(solution)/shard_map/ppermute | solution.py:244
  28.6 3.3 %collective-permute-start.5 = (f32[1,136,128]{2,1,0:T(8,128)S(1)}, f32[1,136,128]{2,1,0:T(8,128)S(1)}, u32[]{:S(2)}, u32[]{:S(2)}) collective-permute-start(f32[1,136,128]{2,1,0:T(8,128)S(1)} %get-tuple-element.38), channel_id=1, source_target_pairs={{0,10},{1,11},{2,8},{3,9},{4,14},{5,15},{6,12},{7,13},{8,2},{9,3},... | collective-permute-start | bytes 208904 | tf_op jit(solution)/shard_map/ppermute | solution.py:244
  31.9 0.9 %collective-permute-start.4 = (f32[1,136,128]{2,1,0:T(8,128)S(1)}, f32[1,136,128]{2,1,0:T(8,128)S(1)}, u32[]{:S(2)}, u32[]{:S(2)}) collective-permute-start(f32[1,136,128]{2,1,0:T(8,128)S(1)} %get-tuple-element.39), channel_id=1, source_target_pairs={{0,8},{1,9},{2,10},{3,11},{4,12},{5,13},{6,14},{7,15},{8,0},{9,1},... | collective-permute-start | bytes 208904 | tf_op jit(solution)/shard_map/ppermute | solution.py:244
  33.2 0.9 %collective-permute-start.10 = (f32[1,136,128]{2,1,0:T(8,128)S(1)}, f32[1,136,128]{2,1,0:T(8,128)S(1)}, u32[]{:S(2)}, u32[]{:S(2)}) collective-permute-start(f32[1,136,128]{2,1,0:T(8,128)S(1)} %get-tuple-element.42), channel_id=1, source_target_pairs={{0,2},{1,3},{2,0},{3,1},{4,6},{5,7},{6,4},{7,5},{8,10},{9,11},{10,... | collective-permute-start | bytes 208904 | tf_op jit(solution)/shard_map/ppermute | solution.py:244
  34.5 3.0 %collective-permute-done.5.refs_3_ = f32[1,136,128]{2,1,0:T(8,128)S(1)} collective-permute-done((f32[1,136,128]{2,1,0:T(8,128)S(1)}, f32[1,136,128]{2,1,0:T(8,128)S(1)}, u32[]{:S(2)}, u32[]{:S(2)}) %collective-permute-start.5) | collective-permute-done | bytes 69664 | tf_op jit(solution)/shard_map/ppermute | solution.py:244
  37.5 1.7 %collective-permute-done.4.refs_2_ = f32[1,136,128]{2,1,0:T(8,128)S(1)} collective-permute-done((f32[1,136,128]{2,1,0:T(8,128)S(1)}, f32[1,136,128]{2,1,0:T(8,128)S(1)}, u32[]{:S(2)}, u32[]{:S(2)}) %collective-permute-start.4) | collective-permute-done | bytes 69664 | tf_op jit(solution)/shard_map/ppermute | solution.py:244
  39.9 7.9 %factor.1.refs_0_ = f32[1,136,128]{2,1,0:T(8,128)S(1)} custom-call(s32[32]{0:T(128)S(1)} %copy-done, f32[32]{0:T(128)S(1)} %copy-done.1, f32[1,136,128]{2,1,0:T(8,128)S(1)} %collective-permute-done.1.refs_0_, f32[1,136,128]{2,1,0:T(8,128)S(1)} %collective-permute-done.2.refs_1_, f32[1,136,128]{2,1,0:T(8,128)S(1)} %collective-permute-done.4.refs_2_, ...), custom_call_target="tpu_custom_call" | custom-call | tf_op jit(solution)/shard_map/factor/pallas_call | solution.py:291
  47.8 1.1 %collective-permute-start.14 = (f32[1,136,128]{2,1,0:T(8,128)S(1)}, f32[1,136,128]{2,1,0:T(8,128)S(1)}, u32[]{:S(2)}, u32[]{:S(2)}) collective-permute-start(f32[1,136,128]{2,1,0:T(8,128)S(1)} %factor.1.refs_0_), channel_id=1, source_target_pairs={{0,2},{1,3},{2,0},{3,1},{4,6},{5,7},{6,4},{7,5},{8,10},{9,11},{10,... | collective-permute-start | bytes 208904 | tf_op jit(solution)/shard_map/ppermute | solution.py:244
  48.9 2.7 %collective-permute-start.12 = (f32[1,136,128]{2,1,0:T(8,128)S(1)}, f32[1,136,128]{2,1,0:T(8,128)S(1)}, u32[]{:S(2)}, u32[]{:S(2)}) collective-permute-start(f32[1,136,128]{2,1,0:T(8,128)S(1)} %factor.1.refs_0_), channel_id=1, source_target_pairs={{0,4},{1,5},{2,6},{3,7},{4,0},{5,1},{6,2},{7,3},{8,12},{9,13},{10,... | collective-permute-start | bytes 208904 | tf_op jit(solution)/shard_map/ppermute | solution.py:244
  51.6 1.8 %collective-permute-done.11.refs_1_ = f32[1,136,128]{2,1,0:T(8,128)S(1)} collective-permute-done((f32[1,136,128]{2,1,0:T(8,128)S(1)}, f32[1,136,128]{2,1,0:T(8,128)S(1)}, u32[]{:S(2)}, u32[]{:S(2)}) %collective-permute-start.11) | collective-permute-done | bytes 69664 | tf_op jit(solution)/shard_map/ppermute | solution.py:244
  54.1 1.2 %collective-permute-start.16 = (f32[1,136,128]{2,1,0:T(8,128)S(1)}, f32[1,136,128]{2,1,0:T(8,128)S(1)}, u32[]{:S(2)}, u32[]{:S(2)}) collective-permute-start(f32[1,136,128]{2,1,0:T(8,128)S(1)} %collective-permute-done.12.refs_2_), channel_id=1, source_target_pairs={{0,2},{1,3},{2,0},{3,1},{4,6},{5,7},{6,4},{7,5},{8,10},{9,11},{10,... | collective-permute-start | bytes 208904 | tf_op jit(solution)/shard_map/ppermute | solution.py:244
  55.3 0.8 %collective-permute-start.15 = (f32[1,136,128]{2,1,0:T(8,128)S(1)}, f32[1,136,128]{2,1,0:T(8,128)S(1)}, u32[]{:S(2)}, u32[]{:S(2)}) collective-permute-start(f32[1,136,128]{2,1,0:T(8,128)S(1)} %collective-permute-done.11.refs_1_), channel_id=1, source_target_pairs={{0,2},{1,3},{2,0},{3,1},{4,6},{5,7},{6,4},{7,5},{8,10},{9,11},{10,... | collective-permute-start | bytes 208904 | tf_op jit(solution)/shard_map/ppermute | solution.py:244
  56.1 1.5 %collective-permute-done.13.refs_3_ = f32[1,136,128]{2,1,0:T(8,128)S(1)} collective-permute-done((f32[1,136,128]{2,1,0:T(8,128)S(1)}, f32[1,136,128]{2,1,0:T(8,128)S(1)}, u32[]{:S(2)}, u32[]{:S(2)}) %collective-permute-start.13) | collective-permute-done | bytes 69664 | tf_op jit(solution)/shard_map/ppermute | solution.py:244
  59.1 1.5 %collective-permute-done.15.refs_5_ = f32[1,136,128]{2,1,0:T(8,128)S(1)} collective-permute-done((f32[1,136,128]{2,1,0:T(8,128)S(1)}, f32[1,136,128]{2,1,0:T(8,128)S(1)}, u32[]{:S(2)}, u32[]{:S(2)}) %collective-permute-start.15) | collective-permute-done | bytes 69664 | tf_op jit(solution)/shard_map/ppermute | solution.py:244
  60.6 1.3 %collective-permute-done.17.refs_7_ = f32[1,136,128]{2,1,0:T(8,128)S(1)} collective-permute-done((f32[1,136,128]{2,1,0:T(8,128)S(1)}, f32[1,136,128]{2,1,0:T(8,128)S(1)}, u32[]{:S(2)}, u32[]{:S(2)}) %collective-permute-start.17) | collective-permute-done | bytes 69664 | tf_op jit(solution)/shard_map/ppermute | solution.py:244
  63.2 3.2 %eliminate.1 = (f32[1,128,128]{2,1,0:T(8,128)}, f32[1,128]{1,0:T(1,128)}) custom-call(f32[1,136,128]{2,1,0:T(8,128)S(1)} %factor.1.refs_0_, f32[1,136,128]{2,1,0:T(8,128)S(1)} %collective-permute-done.11.refs_1_, f32[1,136,128]{2,1,0:T(8,128)S(1)} %collective-permute-done.12.refs_2_, f32[1,136,128]{2,1,0:T(8,128)S(1)} %collective-permute-done.13.refs_3_, ...), custom_call_target="tpu_custom_call" | custom-call | tf_op jit(solution)/shard_map/eliminate/pallas_call | solution.py:304
  (51 shorter events, 7.9 us)
Async XLA Ops:
  8.4 11.8 %collective-permute-start = (f32[2,136,128]{2,1,0:T(8,128)S(1)}, f32[2,136,128]{2,1,0:T(8,128)S(1)}, u32[]{:S(2)}, u32[]{:S(2)}) collective-permute-start(f32[2,136,128]{2,1,0:T(8,128)S(1)} %get-tuple-element.23), channel_id=1, source_target_pairs={{0,1},{1,0},{2,3},{3,2},{4,5},{5,4},{6,7},{7,6},{8,9},{9,8},{10,11... | collective-permute-start | bytes 417800 | tf_op jit(solution)/shard_map/ppermute | solution.py:244
  12.2 14.4 %collective-permute-start.6 = (f32[2,136,128]{2,1,0:T(8,128)S(1)}, f32[2,136,128]{2,1,0:T(8,128)S(1)}, u32[]{:S(2)}, u32[]{:S(2)}) collective-permute-start(f32[2,136,128]{2,1,0:T(8,128)S(1)} %get-tuple-element.27), channel_id=1, source_target_pairs={{0,1},{1,0},{2,3},{3,2},{4,5},{5,4},{6,7},{7,6},{8,9},{9,8},{10,11... | collective-permute-start | bytes 417800 | tf_op jit(solution)/shard_map/ppermute | solution.py:244
  15.5 11.2 %collective-permute-start.3 = (f32[2,136,128]{2,1,0:T(8,128)S(1)}, f32[2,136,128]{2,1,0:T(8,128)S(1)}, u32[]{:S(2)}, u32[]{:S(2)}) collective-permute-start(f32[2,136,128]{2,1,0:T(8,128)S(1)} %get-tuple-element.25), channel_id=1, source_target_pairs={{0,1},{1,0},{2,3},{3,2},{4,5},{5,4},{6,7},{7,6},{8,9},{9,8},{10,11... | collective-permute-start | bytes 417800 | tf_op jit(solution)/shard_map/ppermute | solution.py:244
  20.2 8.4 %collective-permute-start.9 = (f32[2,136,128]{2,1,0:T(8,128)S(1)}, f32[2,136,128]{2,1,0:T(8,128)S(1)}, u32[]{:S(2)}, u32[]{:S(2)}) collective-permute-start(f32[2,136,128]{2,1,0:T(8,128)S(1)} %get-tuple-element.29), channel_id=1, source_target_pairs={{0,1},{1,0},{2,3},{3,2},{4,5},{5,4},{6,7},{7,6},{8,9},{9,8},{10,11... | collective-permute-start | bytes 417800 | tf_op jit(solution)/shard_map/ppermute | solution.py:244
  20.3 11.6 %collective-permute-start.2 = (f32[1,136,128]{2,1,0:T(8,128)S(1)}, f32[1,136,128]{2,1,0:T(8,128)S(1)}, u32[]{:S(2)}, u32[]{:S(2)}) collective-permute-start(f32[1,136,128]{2,1,0:T(8,128)S(1)} %get-tuple-element.40), channel_id=1, source_target_pairs={{0,14},{1,15},{2,12},{3,13},{4,10},{5,11},{6,8},{7,9},{8,6},{9,7},... | collective-permute-start | bytes 208904 | tf_op jit(solution)/shard_map/ppermute | solution.py:244
  26.4 6.9 %collective-permute-start.1 = (f32[1,136,128]{2,1,0:T(8,128)S(1)}, f32[1,136,128]{2,1,0:T(8,128)S(1)}, u32[]{:S(2)}, u32[]{:S(2)}) collective-permute-start(f32[1,136,128]{2,1,0:T(8,128)S(1)} %get-tuple-element.41), channel_id=1, source_target_pairs={{0,12},{1,13},{2,14},{3,15},{4,8},{5,9},{6,10},{7,11},{8,4},{9,5},... | collective-permute-start | bytes 208904 | tf_op jit(solution)/shard_map/ppermute | solution.py:244
  26.6 7.9 %collective-permute-start.8 = (f32[1,136,128]{2,1,0:T(8,128)S(1)}, f32[1,136,128]{2,1,0:T(8,128)S(1)}, u32[]{:S(2)}, u32[]{:S(2)}) collective-permute-start(f32[1,136,128]{2,1,0:T(8,128)S(1)} %get-tuple-element.36), channel_id=1, source_target_pairs={{0,6},{1,7},{2,4},{3,5},{4,2},{5,3},{6,0},{7,1},{8,14},{9,15},{10,... | collective-permute-start | bytes 208904 | tf_op jit(solution)/shard_map/ppermute | solution.py:244
  26.7 7.8 %collective-permute-start.7 = (f32[1,136,128]{2,1,0:T(8,128)S(1)}, f32[1,136,128]{2,1,0:T(8,128)S(1)}, u32[]{:S(2)}, u32[]{:S(2)}) collective-permute-start(f32[1,136,128]{2,1,0:T(8,128)S(1)} %get-tuple-element.37), channel_id=1, source_target_pairs={{0,4},{1,5},{2,6},{3,7},{4,0},{5,1},{6,2},{7,3},{8,12},{9,13},{10,... | collective-permute-start | bytes 208904 | tf_op jit(solution)/shard_map/ppermute | solution.py:244
  28.6 8.9 %collective-permute-start.5 = (f32[1,136,128]{2,1,0:T(8,128)S(1)}, f32[1,136,128]{2,1,0:T(8,128)S(1)}, u32[]{:S(2)}, u32[]{:S(2)}) collective-permute-start(f32[1,136,128]{2,1,0:T(8,128)S(1)} %get-tuple-element.38), channel_id=1, source_target_pairs={{0,10},{1,11},{2,8},{3,9},{4,14},{5,15},{6,12},{7,13},{8,2},{9,3},... | collective-permute-start | bytes 208904 | tf_op jit(solution)/shard_map/ppermute | solution.py:244
  31.9 7.3 %collective-permute-start.4 = (f32[1,136,128]{2,1,0:T(8,128)S(1)}, f32[1,136,128]{2,1,0:T(8,128)S(1)}, u32[]{:S(2)}, u32[]{:S(2)}) collective-permute-start(f32[1,136,128]{2,1,0:T(8,128)S(1)} %get-tuple-element.39), channel_id=1, source_target_pairs={{0,8},{1,9},{2,10},{3,11},{4,12},{5,13},{6,14},{7,15},{8,0},{9,1},... | collective-permute-start | bytes 208904 | tf_op jit(solution)/shard_map/ppermute | solution.py:244
  33.2 6.0 %collective-permute-start.10 = (f32[1,136,128]{2,1,0:T(8,128)S(1)}, f32[1,136,128]{2,1,0:T(8,128)S(1)}, u32[]{:S(2)}, u32[]{:S(2)}) collective-permute-start(f32[1,136,128]{2,1,0:T(8,128)S(1)} %get-tuple-element.42), channel_id=1, source_target_pairs={{0,2},{1,3},{2,0},{3,1},{4,6},{5,7},{6,4},{7,5},{8,10},{9,11},{10,... | collective-permute-start | bytes 208904 | tf_op jit(solution)/shard_map/ppermute | solution.py:244
  47.8 5.5 %collective-permute-start.11 = (f32[1,136,128]{2,1,0:T(8,128)S(1)}, f32[1,136,128]{2,1,0:T(8,128)S(1)}, u32[]{:S(2)}, u32[]{:S(2)}) collective-permute-start(f32[1,136,128]{2,1,0:T(8,128)S(1)} %factor.1.refs_0_), channel_id=1, source_target_pairs={{0,8},{1,9},{2,10},{3,11},{4,12},{5,13},{6,14},{7,15},{8,0},{9,1},... | collective-permute-start | bytes 208904 | tf_op jit(solution)/shard_map/ppermute | solution.py:244
  47.8 5.5 %collective-permute-start.14 = (f32[1,136,128]{2,1,0:T(8,128)S(1)}, f32[1,136,128]{2,1,0:T(8,128)S(1)}, u32[]{:S(2)}, u32[]{:S(2)}) collective-permute-start(f32[1,136,128]{2,1,0:T(8,128)S(1)} %factor.1.refs_0_), channel_id=1, source_target_pairs={{0,2},{1,3},{2,0},{3,1},{4,6},{5,7},{6,4},{7,5},{8,10},{9,11},{10,... | collective-permute-start | bytes 208904 | tf_op jit(solution)/shard_map/ppermute | solution.py:244
  48.9 5.2 %collective-permute-start.12 = (f32[1,136,128]{2,1,0:T(8,128)S(1)}, f32[1,136,128]{2,1,0:T(8,128)S(1)}, u32[]{:S(2)}, u32[]{:S(2)}) collective-permute-start(f32[1,136,128]{2,1,0:T(8,128)S(1)} %factor.1.refs_0_), channel_id=1, source_target_pairs={{0,4},{1,5},{2,6},{3,7},{4,0},{5,1},{6,2},{7,3},{8,12},{9,13},{10,... | collective-permute-start | bytes 208904 | tf_op jit(solution)/shard_map/ppermute | solution.py:244
  51.6 3.7 %collective-permute-start.18 = (f32[1,136,128]{2,1,0:T(8,128)S(1)}, f32[1,136,128]{2,1,0:T(8,128)S(1)}, u32[]{:S(2)}, u32[]{:S(2)}) collective-permute-start(f32[1,136,128]{2,1,0:T(8,128)S(1)} %factor.1.refs_0_), channel_id=1, source_target_pairs={{0,1},{1,0},{2,3},{3,2},{4,5},{5,4},{6,7},{7,6},{8,9},{9,8},{10,11... | collective-permute-start | bytes 208904 | tf_op jit(solution)/shard_map/ppermute | solution.py:244
  53.3 4.3 %collective-permute-start.13 = (f32[1,136,128]{2,1,0:T(8,128)S(1)}, f32[1,136,128]{2,1,0:T(8,128)S(1)}, u32[]{:S(2)}, u32[]{:S(2)}) collective-permute-start(f32[1,136,128]{2,1,0:T(8,128)S(1)} %collective-permute-done.11.refs_1_), channel_id=1, source_target_pairs={{0,4},{1,5},{2,6},{3,7},{4,0},{5,1},{6,2},{7,3},{8,12},{9,13},{10,... | collective-permute-start | bytes 208904 | tf_op jit(solution)/shard_map/ppermute | solution.py:244
  53.3 5.0 %collective-permute-start.22 = (f32[1,136,128]{2,1,0:T(8,128)S(1)}, f32[1,136,128]{2,1,0:T(8,128)S(1)}, u32[]{:S(2)}, u32[]{:S(2)}) collective-permute-start(f32[1,136,128]{2,1,0:T(8,128)S(1)} %collective-permute-done.14.refs_4_), channel_id=1, source_target_pairs={{0,1},{1,0},{2,3},{3,2},{4,5},{5,4},{6,7},{7,6},{8,9},{9,8},{10,11... | collective-permute-start | bytes 208904 | tf_op jit(solution)/shard_map/ppermute | solution.py:244
  54.1 4.3 %collective-permute-start.20 = (f32[1,136,128]{2,1,0:T(8,128)S(1)}, f32[1,136,128]{2,1,0:T(8,128)S(1)}, u32[]{:S(2)}, u32[]{:S(2)}) collective-permute-start(f32[1,136,128]{2,1,0:T(8,128)S(1)} %collective-permute-done.12.refs_2_), channel_id=1, source_target_pairs={{0,1},{1,0},{2,3},{3,2},{4,5},{5,4},{6,7},{7,6},{8,9},{9,8},{10,11... | collective-permute-start | bytes 208904 | tf_op jit(solution)/shard_map/ppermute | solution.py:244
  54.1 5.1 %collective-permute-start.16 = (f32[1,136,128]{2,1,0:T(8,128)S(1)}, f32[1,136,128]{2,1,0:T(8,128)S(1)}, u32[]{:S(2)}, u32[]{:S(2)}) collective-permute-start(f32[1,136,128]{2,1,0:T(8,128)S(1)} %collective-permute-done.12.refs_2_), channel_id=1, source_target_pairs={{0,2},{1,3},{2,0},{3,1},{4,6},{5,7},{6,4},{7,5},{8,10},{9,11},{10,... | collective-permute-start | bytes 208904 | tf_op jit(solution)/shard_map/ppermute | solution.py:244
  55.3 5.3 %collective-permute-start.15 = (f32[1,136,128]{2,1,0:T(8,128)S(1)}, f32[1,136,128]{2,1,0:T(8,128)S(1)}, u32[]{:S(2)}, u32[]{:S(2)}) collective-permute-start(f32[1,136,128]{2,1,0:T(8,128)S(1)} %collective-permute-done.11.refs_1_), channel_id=1, source_target_pairs={{0,2},{1,3},{2,0},{3,1},{4,6},{5,7},{6,4},{7,5},{8,10},{9,11},{10,... | collective-permute-start | bytes 208904 | tf_op jit(solution)/shard_map/ppermute | solution.py:244
  57.6 4.3 %collective-permute-start.17 = (f32[1,136,128]{2,1,0:T(8,128)S(1)}, f32[1,136,128]{2,1,0:T(8,128)S(1)}, u32[]{:S(2)}, u32[]{:S(2)}) collective-permute-start(f32[1,136,128]{2,1,0:T(8,128)S(1)} %collective-permute-done.13.refs_3_), channel_id=1, source_target_pairs={{0,2},{1,3},{2,0},{3,1},{4,6},{5,7},{6,4},{7,5},{8,10},{9,11},{10,... | collective-permute-start | bytes 208904 | tf_op jit(solution)/shard_map/ppermute | solution.py:244
  58.4 4.2 %collective-permute-start.19 = (f32[1,136,128]{2,1,0:T(8,128)S(1)}, f32[1,136,128]{2,1,0:T(8,128)S(1)}, u32[]{:S(2)}, u32[]{:S(2)}) collective-permute-start(f32[1,136,128]{2,1,0:T(8,128)S(1)} %collective-permute-done.11.refs_1_), channel_id=1, source_target_pairs={{0,1},{1,0},{2,3},{3,2},{4,5},{5,4},{6,7},{7,6},{8,9},{9,8},{10,11... | collective-permute-start | bytes 208904 | tf_op jit(solution)/shard_map/ppermute | solution.py:244
  58.4 4.2 %collective-permute-start.21 = (f32[1,136,128]{2,1,0:T(8,128)S(1)}, f32[1,136,128]{2,1,0:T(8,128)S(1)}, u32[]{:S(2)}, u32[]{:S(2)}) collective-permute-start(f32[1,136,128]{2,1,0:T(8,128)S(1)} %collective-permute-done.13.refs_3_), channel_id=1, source_target_pairs={{0,1},{1,0},{2,3},{3,2},{4,5},{5,4},{6,7},{7,6},{8,9},{9,8},{10,11... | collective-permute-start | bytes 208904 | tf_op jit(solution)/shard_map/ppermute | solution.py:244
  59.1 3.4 %collective-permute-start.24 = (f32[1,136,128]{2,1,0:T(8,128)S(1)}, f32[1,136,128]{2,1,0:T(8,128)S(1)}, u32[]{:S(2)}, u32[]{:S(2)}) collective-permute-start(f32[1,136,128]{2,1,0:T(8,128)S(1)} %collective-permute-done.16.refs_6_), channel_id=1, source_target_pairs={{0,1},{1,0},{2,3},{3,2},{4,5},{5,4},{6,7},{7,6},{8,9},{9,8},{10,11... | collective-permute-start | bytes 208904 | tf_op jit(solution)/shard_map/ppermute | solution.py:244
  (8 other events, 8.4 us)

commit v2 on v1

--- a/solution.py
+++ b/solution.py
@@ -27,22 +27,46 @@
     lax.fori_loop(0, arcs, put, 0)
 
 
-def tiles_kernel(owners, want_table, want_own, *refs):
-    slot_ref, id_ref, miss_ref, stn_rows_ref, arc_rows_ref = refs[:5]
-    table_ref, sent_ref, kept_ref, cross_ref = refs[5:9]
-    own_ref = refs[9] if want_own else None
-    arc_ref, ids_sc = refs[-2:]
-    rows, width = arc_rows_ref.shape
+def tiles_kernel(owners, first, last, *refs):
+    if first:
+        slot_any, id_any, miss_any, stn_any, arc_any = refs[:5]
+        table_ref, rows_ref, sent_ref, kept_ref, cross_ref = refs[5:10]
+        arc_ref, ids_sc, slot_ref, id_ref, miss_ref, sems = refs[10:]
+        width = arc_any.shape[1]
+        moves = [
+            pltpu.make_async_copy(source, target, sems.at[at])
+            for at, (source, target) in enumerate(
+                [
+                    (slot_any, slot_ref),
+                    (arc_any, rows_ref.at[:, pl.ds(0, width)]),
+                    (id_any, id_ref),
+                    (miss_any, miss_ref),
+                    (stn_any, rows_ref.at[:, pl.ds(width, width)]),
+                ]
+            )
+        ]
+        for move in moves:
+            move.start()
+    else:
+        slot_ref, id_ref, miss_ref, table_ref, rows_ref = refs[:5]
+        prior_ref = refs[5] if last else None
+        sent_ref, kept_ref, cross_ref, arc_ref, ids_sc = refs[-5:]
+    rows, width = rows_ref.shape[0], rows_ref.shape[1] // 2
     arcs = slot_ref.shape[0]
     me = lax.axis_index("stn")
+    if first:
+        moves[0].wait()
     arcs_of_slots(slot_ref, arc_ref, arcs)
+    if first:
+        moves[1].wait()
+        table_ref[...] = rows_ref[:, 0:width].T
+        for move in moves[2:]:
+            move.wait()
     ids_sc[...] = jnp.broadcast_to(id_ref[...].astype(jnp.float32), ids_sc.shape)
-    if want_table:
-        table_ref[...] = arc_rows_ref[...].T
     mine = []
     for owner in owners:
-        first = 2 * jnp.bitwise_xor(me, owner)
-        mine += [arc_ref[first], arc_ref[first + 1]]
+        slot = 2 * jnp.bitwise_xor(me, owner)
+        mine += [arc_ref[slot], arc_ref[slot + 1]]
     sub16 = lax.broadcasted_iota(jnp.int32, ids_sc.shape, 0)
     named = jnp.full(ids_sc.shape, -1.0, jnp.float32)
     left = []
@@ -56,9 +80,8 @@
     miss = miss_ref[...].astype(jnp.float32)
     miss = jnp.concatenate([miss[at : at + 1] for at in range(miss.shape[0])], axis=1)
     left.append(hit * jnp.broadcast_to(miss, hit.shape).astype(jnp.bfloat16))
-    right = jnp.concatenate([arc_rows_ref[...], stn_rows_ref[...]], axis=1)
     full = lax.dot_general(
-        jnp.concatenate(left, axis=0), right, NN, preferred_element_type=jnp.float32
+        jnp.concatenate(left, axis=0), rows_ref[...], NN, preferred_element_type=jnp.float32
     )
     r = lax.broadcasted_iota(jnp.int32, (width, width), 0)
     c = lax.broadcasted_iota(jnp.int32, (width, width), 1)
@@ -67,21 +90,26 @@
     half = len(owners) // 2
     for at in range(len(owners)):
         top = 2 * at * width
-        first, second = full[top : top + width, :width], full[top + width : top + 2 * width, :width]
+        lower, upper = full[top : top + width, :width], full[top + width : top + 2 * width, :width]
         out_ref = sent_ref if at < half else kept_ref
-        out_ref[at % half, 0:width, :] = jnp.where(r >= c, first, second)
-        diag = jnp.sum(jnp.where(r == c, second, 0.0), axis=0, keepdims=True)
+        out_ref[at % half, 0:width, :] = jnp.where(r >= c, lower, upper)
+        diag = jnp.sum(jnp.where(r == c, upper, 0.0), axis=0, keepdims=True)
         tail = jnp.where(sub == 0, diag, 0.0)
         tail = jnp.where(sub == 1, rights[2 * at : 2 * at + 1], tail)
-        out_ref[at % half, width:, :] = jnp.where(sub == 2, rights[2 * at + 1 : 2 * at + 2], tail)
+        tail = jnp.where(sub == 2, rights[2 * at + 1 : 2 * at + 2], tail)
+        if last and owners[at] == 0:
+            for side in range(2):
+                tail = jnp.where(sub == 3 + side, prior_ref[mine[2 * at + side]] * rows, tail)
+        out_ref[at % half, width:, :] = tail
         for side in range(2):
             cross = full[top + side * width : top + (side + 1) * width, width:]
             cross_ref[2 * at + side, :, :width], cross_ref[2 * at + side, :, width:] = split(cross)
-    if want_own:
-        own = lax.dot_general(
-            stn_rows_ref[...].T, stn_rows_ref[...], NN, preferred_element_type=jnp.float32
-        )
-        own_ref[0] = own / rows
+
+
+def own_kernel(rows_ref, out_ref):
+    rows = rows_ref[...]
+    own = lax.dot_general(rows.T, rows, NN, preferred_element_type=jnp.float32)
+    out_ref[0] = own / rows.shape[0]
 
 
 def lanes_of(block, k):
@@ -134,21 +162,9 @@
         tile[t] = rest
 
 
-def factor_kernel(rows, slot_ref, prior_ref, *refs):
+def factor_kernel(*refs):
     (out_ref, sys_sc), terms = refs[-2:], refs[:-2]
     width = out_ref.shape[-1]
-    arcs = slot_ref.shape[0]
-    me = lax.axis_index("stn")
-
-    def find(arc, found):
-        hit = slot_ref[arc]
-        weight = prior_ref[arc]
-        return (
-            jnp.where(hit == 2 * me, weight, found[0]),
-            jnp.where(hit == 2 * me + 1, weight, found[1]),
-        )
-
-    priors = lax.fori_loop(0, arcs, find, (jnp.float32(0), jnp.float32(0)))
     whole = sum([term[0] for term in terms[1:]], terms[0][0])
     packed, tail = whole[:width], whole[width:]
     flipped = packed.T
@@ -158,8 +174,8 @@
     first = jnp.where(r >= c, packed, flipped)
     second = jnp.where(r < c, packed, flipped)
     second = jnp.where(eye, tail[0:1, :], second)
-    sys_sc[0] = first + jnp.where(eye, priors[0] * rows, 0.0)
-    sys_sc[1] = second + jnp.where(eye, priors[1] * rows, 0.0)
+    sys_sc[0] = first + jnp.where(eye, tail[3:4, :], 0.0)
+    sys_sc[1] = second + jnp.where(eye, tail[4:5, :], 0.0)
     tiles = width // 8
     sub = lax.broadcasted_iota(jnp.int32, (8, width), 0)
     lane = lax.broadcasted_iota(jnp.int32, (8, width), 1)
@@ -184,10 +200,14 @@
     out_ref[0, width:, :] = jnp.where(sub == 2, whitened[1], last)
 
 
-def eliminate_kernel(places, *refs):
+def eliminate_kernel(places, added, last, *refs):
     pieces, refs = refs[: len(places)], refs[len(places) :]
-    crosses, (elim_ref, rhs_ref, sum_sc) = refs[:-3], refs[-3:]
-    width = elim_ref.shape[1]
+    before, refs = refs[:added], refs[added:]
+    if last:
+        crosses, (elim_ref, rhs_ref, sum_sc) = refs[:-3], refs[-3:]
+    else:
+        crosses, sum_sc = refs[:-1], refs[-1]
+    width = sum_sc.shape[1] // 2
     r = lax.broadcasted_iota(jnp.int32, (width, width), 0)
     c = lax.broadcasted_iota(jnp.int32, (width, width), 1)
     rows16 = lax.broadcasted_iota(jnp.int32, (16, 2 * width), 0)
@@ -220,7 +240,9 @@
         if count:
             sum_sc[...] += term
         else:
-            sum_sc[...] = term
+            sum_sc[...] = sum([ref[...] for ref in before], term)
+    if not last:
+        return
     total = sum_sc[...]
     mixed = total[:width, width:]
     elim_ref[0] = (total[:width, :width] + (mixed + mixed.T)) / width
@@ -248,25 +270,40 @@
     for chunk in range(chunks):
         far = groups - 4 * (chunk + 1)
         owners = [far + 1, far + 3, far, far + 2]
-        want_own = chunk == chunks - 1
         shapes = [
             jax.ShapeDtypeStruct((2, tall, width), f32),
             jax.ShapeDtypeStruct((2, tall, width), f32),
             jax.ShapeDtypeStruct((2 * len(owners), width, 2 * width), bf16),
         ]
-        if chunk == 0:
-            shapes.insert(0, jax.ShapeDtypeStruct((width, rows), bf16))
-        if want_own:
-            shapes.append(jax.ShapeDtypeStruct((1, width, width), f32))
-        operands = [arc_slot, ids, miss, station_partials, arc_partials]
-        if chunk:
-            operands.append(table)
+        scratch = [pltpu.SMEM((arcs,), jnp.int32), pltpu.VMEM((16, rows), f32)]
+        first, last = chunk == 0, chunk == chunks - 1
+        if first:
+            shapes = [
+                jax.ShapeDtypeStruct((width, rows), bf16),
+                jax.ShapeDtypeStruct((rows, 2 * width), bf16),
+            ] + shapes
+            scratch += [
+                pltpu.SMEM((arcs,), jnp.int32),
+                pltpu.VMEM(ids.shape, ids.dtype),
+                pltpu.VMEM(miss.shape, miss.dtype),
+                pltpu.SemaphoreType.DMA((5,)),
+            ]
+            held = [arc_slot, ids, miss, station_partials, arc_partials]
+            held = [pltpu.with_memory_space_constraint(value, pltpu.HBM) for value in held]
+            operands = held
+            in_specs = [pl.BlockSpec(memory_space=pltpu.HBM)] * 5
+        else:
+            operands = [arc_slot, ids, miss, *shared]
+            in_specs = [smem] + [vmem] * 4
+            if last:
+                operands.append(arc_prior)
+                in_specs.append(smem)
         found = pl.pallas_call(
-            functools.partial(tiles_kernel, tuple(owners), chunk == 0, want_own),
+            functools.partial(tiles_kernel, tuple(owners), first, last),
             out_shape=shapes,
-            in_specs=[smem] + [vmem] * (len(operands) - 1),
+            in_specs=in_specs,
             out_specs=[vmem] * len(shapes),
-            scratch_shapes=[pltpu.SMEM((arcs,), jnp.int32), pltpu.VMEM((16, rows), f32)],
+            scratch_shapes=scratch,
             cost_estimate=pl.CostEstimate(
                 flops=2 * rows * 2 * len(owners) * width * 2 * width,
                 bytes_accessed=4 * rows * width,
@@ -275,9 +312,9 @@
             compiler_params=LIMITED,
             name="tiles",
         )(*operands)
-        if chunk == 0:
-            table, found = found[0], found[1:]
-        sent, kept, cross, *own = found
+        if first:
+            shared, found = found[:2], found[2:]
+        sent, kept, cross = found
         crosses.append(cross)
         where.update({owner: (chunk, at) for at, owner in enumerate(owners)})
         came = swap(sent, 1)
@@ -287,32 +324,56 @@
                 terms.append(swap(both, owner))
             else:
                 terms += [kept[at : at + 1], came[at : at + 1]]
-    (station_normal,) = own
     mine = pl.pallas_call(
-        functools.partial(factor_kernel, float(rows)),
+        factor_kernel,
         out_shape=jax.ShapeDtypeStruct((1, tall, width), f32),
-        in_specs=[smem, smem] + [vmem] * len(terms),
+        in_specs=[vmem] * len(terms),
         out_specs=vmem,
         scratch_shapes=[pltpu.VMEM((2, width, width), f32)],
         compiler_params=LIMITED,
         name="factor",
-    )(arc_slot, arc_prior, *terms)
+    )(*terms)
     arc_whitened = mine[0, width + 1 : width + 3, :]
     pieces = {0: mine}
     for bit in reversed(range(bits)):
-        pieces.update({owner ^ (1 << bit): swap(piece, 1 << bit) for owner, piece in pieces.items()})
+        came = {}
+        for owner, piece in pieces.items():
+            came[owner ^ (1 << bit)] = swap(piece, 1 << bit)
+        pieces.update(came)
+    station_normal = pl.pallas_call(
+        own_kernel,
+        out_shape=jax.ShapeDtypeStruct((1, width, width), f32),
+        in_specs=[vmem],
+        out_specs=vmem,
+        compiler_params=LIMITED,
+        name="own",
+    )(station_partials)
+    late = list(pieces)[-1]
+    soon = [owner for owner in pieces if not owner & 2]
+    then = [owner for owner in pieces if owner & 2 and owner != late]
+    before = []
+    for group in (soon, then):
+        before = [
+            pl.pallas_call(
+                functools.partial(eliminate_kernel, tuple(where[owner] for owner in group), len(before), False),
+                out_shape=jax.ShapeDtypeStruct((width + 16, 2 * width), f32),
+                in_specs=[vmem] * (len(group) + len(before) + chunks),
+                out_specs=vmem,
+                compiler_params=LIMITED,
+            )(*[pieces[owner] for owner in group], *before, *crosses)
+        ]
     elimination, elimination_rhs = pl.pallas_call(
-        functools.partial(eliminate_kernel, tuple(where[owner] for owner in pieces)),
+        functools.partial(eliminate_kernel, (where[late],), 1, True),
         out_shape=[
             jax.ShapeDtypeStruct((1, width, width), f32),
             jax.ShapeDtypeStruct((1, width), f32),
         ],
-        in_specs=[vmem] * (len(pieces) + chunks),
+        in_specs=[vmem] * (2 + chunks),
         out_specs=[vmem, vmem],
         scratch_shapes=[pltpu.VMEM((width + 16, 2 * width), f32)],
         compiler_params=LIMITED,
         name="eliminate",
-    )(*pieces.values(), *crosses)
+    )(pieces[late], *before, *crosses)
     return (station_normal, elimination, elimination_rhs, arc_whitened)
 
 

time: 66.8 us -> 61 us (0.913)
  local copies, waits for them, and re-layouts: 5.73 us -> 0.59 us
  waiting for transfers between devices: 13.4 us -> 9.21 us
  starting transfers between devices: 21.5 us -> 24.5 us
  Pallas kernels: 25 us -> 25.7 us
    unnamed x12 -> x10, local copies, waits for them, and re-layouts: 5.17 us -> 0.03 us
    ppermute x26, waiting for transfers between devices: 13.4 us -> 9.21 us  [swap(): return lax.ppermute(value, 'stn', [(at, at ^ flip) for at in range(groups)])]
    ppermute x26, starting transfers between devices: 21.5 us -> 24.5 us  [swap(): return lax.ppermute(value, 'stn', [(at, at ^ flip) for at in range(groups)])]
    pallas_call x5 -> x7, Pallas kernels: 21.8 us -> 23.1 us  [the longest x4 13.8 us: body(): pl.pallas_call(functools.partial(tiles_kernel, tuple(owners), first, last...]
    pallas_call x1 -> x2, Pallas kernels: 3.2 us -> 2.62 us  [body(): pl.pallas_call(functools.partial(eliminate_kernel, tuple((where[owner] fo...]
  transfers between devices with their start and end apart: 26 -> 26, of which waited for: 11 -> 8; matrix products, arithmetic and copies ran while one was open for 1% -> 1% of each run, Pallas kernels for 16% -> 22%
where the time goes in v2:
time: 61 us; the launch traced here: 60.9 us
  Pallas kernels  25.7 us (42%)
  starting transfers between devices  24.5 us (40%)
  waiting for transfers between devices  9.21 us (15%)
  between operations  0.8 us (1%)
    ppermute x26, starting transfers between devices, swap(): return lax.ppermute(value, 'stn', [(at, at ^ flip) for at in range(groups)])  24.5 us
    pallas_call x4, Pallas kernels, body(): pl.pallas_call(functools.partial(tiles_kernel, tuple(owners), first, last...  13.8 us
    ppermute x26, waiting for transfers between devices, swap(): return lax.ppermute(value, 'stn', [(at, at ^ flip) for at in range(groups)])  9.21 us
    pallas_call x1, Pallas kernels, body(): pl.pallas_call(factor_kernel, out_shape=jax.ShapeDtypeStruct((1, tall, wi...  7.01 us
    pallas_call x2, Pallas kernels, body(): pl.pallas_call(functools.partial(eliminate_kernel, tuple((where[owner] fo...  2.62 us
  transfers between devices with their start and end apart: 26, of which 8 were waited for; matrix products, arithmetic and copies ran while one was open for 1% of the time, Pallas kernels for 22%

profile of v2, /device:TPU:0, one launch (start us, length us, event | category | flops | bytes accessed | tf_op | source)
XLA Modules:
  0.0 60.9 jit_solution(3975500812319506778)
XLA Ops:
  0.7 4.0 %tiles.4 = (bf16[128,4096]{1,0:T(8,128)(2,1)S(1)}, bf16[4096,256]{1,0:T(8,128)(2,1)S(1)}, f32[2,136,128]{2,1,0:T(8,128)S(1)}, f32[2,136,128]{2,1,0:T(8,128)S(1)}, bf16[8,128,256]{2,1,0:T(8,128)(2,1)S(1)}) custom-call(s32[32]{0:T(128)} %refs_0_.7, s32[1,4096]{1,0:T(1,128)} %bitcast.4, bf16[32,128]{1,0:T(8,128)(2,1)} %bitcast.8, bf16[4096,128]{1,0:T(8,128)(2,1)} %refs_3_.1, ...), custom_call_target="tpu_custom_call" | custom-call | flops 2147483648 | bytes 2097152 | tf_op jit(solution)/shard_map/tiles/pallas_call | solution.py:301
  5.3 3.2 %tiles.5 = (f32[2,136,128]{2,1,0:T(8,128)S(1)}, f32[2,136,128]{2,1,0:T(8,128)S(1)}, bf16[8,128,256]{2,1,0:T(8,128)(2,1)S(1)}) custom-call(s32[32]{0:T(128)S(1)} %copy-done.3, s32[1,4096]{1,0:T(1,128)S(1)} %bitcast.5, bf16[32,128]{1,0:T(8,128)(2,1)S(1)} %bitcast.9, bf16[128,4096]{1,0:T(8,128)(2,1)S(1)} %get-tuple-element.22.refs_3_, ...), custom_call_target="tpu_custom_call" | custom-call | flops 2147483648 | bytes 2097152 | tf_op jit(solution)/shard_map/tiles/pallas_call | solution.py:301
  8.6 3.2 %tiles.6 = (f32[2,136,128]{2,1,0:T(8,128)S(1)}, f32[2,136,128]{2,1,0:T(8,128)S(1)}, bf16[8,128,256]{2,1,0:T(8,128)(2,1)S(1)}) custom-call(s32[32]{0:T(128)S(1)} %copy-done.3, s32[1,4096]{1,0:T(1,128)S(1)} %bitcast.6, bf16[32,128]{1,0:T(8,128)(2,1)S(1)} %bitcast.10, bf16[128,4096]{1,0:T(8,128)(2,1)S(1)} %get-tuple-element.22.refs_3_, ...), custom_call_target="tpu_custom_call" | custom-call | flops 2147483648 | bytes 2097152 | tf_op jit(solution)/shard_map/tiles/pallas_call | solution.py:301
  12.4 3.4 %tiles.7 = (f32[2,136,128]{2,1,0:T(8,128)S(1)}, f32[2,136,128]{2,1,0:T(8,128)S(1)}, bf16[8,128,256]{2,1,0:T(8,128)(2,1)S(1)}) custom-call(s32[32]{0:T(128)S(1)} %copy-done.3, s32[1,4096]{1,0:T(1,128)S(1)} %bitcast.7, bf16[32,128]{1,0:T(8,128)(2,1)S(1)} %bitcast.11, bf16[128,4096]{1,0:T(8,128)(2,1)S(1)} %get-tuple-element.22.refs_3_, ...), custom_call_target="tpu_custom_call" | custom-call | flops 2147483648 | bytes 2097152 | tf_op jit(solution)/shard_map/tiles/pallas_call | solution.py:301
  15.9 5.1 %collective-permute-start.1 = (f32[1,136,128]{2,1,0:T(8,128)S(1)}, f32[1,136,128]{2,1,0:T(8,128)S(1)}, u32[]{:S(2)}, u32[]{:S(2)}) collective-permute-start(f32[1,136,128]{2,1,0:T(8,128)S(1)} %get-tuple-element.41), channel_id=1, source_target_pairs={{0,12},{1,13},{2,14},{3,15},{4,8},{5,9},{6,10},{7,11},{8,4},{9,5},... | collective-permute-start | bytes 208904 | tf_op jit(solution)/shard_map/ppermute | solution.py:266
  21.0 1.2 %collective-permute-start.2 = (f32[1,136,128]{2,1,0:T(8,128)S(1)}, f32[1,136,128]{2,1,0:T(8,128)S(1)}, u32[]{:S(2)}, u32[]{:S(2)}) collective-permute-start(f32[1,136,128]{2,1,0:T(8,128)S(1)} %get-tuple-element.40), channel_id=1, source_target_pairs={{0,14},{1,15},{2,12},{3,13},{4,10},{5,11},{6,8},{7,9},{8,6},{9,7},... | collective-permute-start | bytes 208904 | tf_op jit(solution)/shard_map/ppermute | solution.py:266
  22.2 0.9 %collective-permute-start.4 = (f32[1,136,128]{2,1,0:T(8,128)S(1)}, f32[1,136,128]{2,1,0:T(8,128)S(1)}, u32[]{:S(2)}, u32[]{:S(2)}) collective-permute-start(f32[1,136,128]{2,1,0:T(8,128)S(1)} %get-tuple-element.39), channel_id=1, source_target_pairs={{0,8},{1,9},{2,10},{3,11},{4,12},{5,13},{6,14},{7,15},{8,0},{9,1},... | collective-permute-start | bytes 208904 | tf_op jit(solution)/shard_map/ppermute | solution.py:266
  23.1 1.9 %collective-permute-start.5 = (f32[1,136,128]{2,1,0:T(8,128)S(1)}, f32[1,136,128]{2,1,0:T(8,128)S(1)}, u32[]{:S(2)}, u32[]{:S(2)}) collective-permute-start(f32[1,136,128]{2,1,0:T(8,128)S(1)} %get-tuple-element.38), channel_id=1, source_target_pairs={{0,10},{1,11},{2,8},{3,9},{4,14},{5,15},{6,12},{7,13},{8,2},{9,3},... | collective-permute-start | bytes 208904 | tf_op jit(solution)/shard_map/ppermute | solution.py:266
  25.0 1.5 %collective-permute-start.7 = (f32[1,136,128]{2,1,0:T(8,128)S(1)}, f32[1,136,128]{2,1,0:T(8,128)S(1)}, u32[]{:S(2)}, u32[]{:S(2)}) collective-permute-start(f32[1,136,128]{2,1,0:T(8,128)S(1)} %get-tuple-element.37), channel_id=1, source_target_pairs={{0,4},{1,5},{2,6},{3,7},{4,0},{5,1},{6,2},{7,3},{8,12},{9,13},{10,... | collective-permute-start | bytes 208904 | tf_op jit(solution)/shard_map/ppermute | solution.py:266
  26.6 2.5 %collective-permute-start.8 = (f32[1,136,128]{2,1,0:T(8,128)S(1)}, f32[1,136,128]{2,1,0:T(8,128)S(1)}, u32[]{:S(2)}, u32[]{:S(2)}) collective-permute-start(f32[1,136,128]{2,1,0:T(8,128)S(1)} %get-tuple-element.36), channel_id=1, source_target_pairs={{0,6},{1,7},{2,4},{3,5},{4,2},{5,3},{6,0},{7,1},{8,14},{9,15},{10,... | collective-permute-start | bytes 208904 | tf_op jit(solution)/shard_map/ppermute | solution.py:266
  29.1 0.8 %collective-permute-start.10 = (f32[1,136,128]{2,1,0:T(8,128)S(1)}, f32[1,136,128]{2,1,0:T(8,128)S(1)}, u32[]{:S(2)}, u32[]{:S(2)}) collective-permute-start(f32[1,136,128]{2,1,0:T(8,128)S(1)} %get-tuple-element.42), channel_id=1, source_target_pairs={{0,2},{1,3},{2,0},{3,1},{4,6},{5,7},{6,4},{7,5},{8,10},{9,11},{10,... | collective-permute-start | bytes 208904 | tf_op jit(solution)/shard_map/ppermute | solution.py:266
  29.9 2.3 %collective-permute-done.4.refs_2_ = f32[1,136,128]{2,1,0:T(8,128)S(1)} collective-permute-done((f32[1,136,128]{2,1,0:T(8,128)S(1)}, f32[1,136,128]{2,1,0:T(8,128)S(1)}, u32[]{:S(2)}, u32[]{:S(2)}) %collective-permute-start.4) | collective-permute-done | bytes 69664 | tf_op jit(solution)/shard_map/ppermute | solution.py:266
  32.2 1.9 %collective-permute-done.5.refs_3_ = f32[1,136,128]{2,1,0:T(8,128)S(1)} collective-permute-done((f32[1,136,128]{2,1,0:T(8,128)S(1)}, f32[1,136,128]{2,1,0:T(8,128)S(1)}, u32[]{:S(2)}, u32[]{:S(2)}) %collective-permute-start.5) | collective-permute-done | bytes 69664 | tf_op jit(solution)/shard_map/ppermute | solution.py:266
  34.6 7.0 %factor.1.refs_0_ = f32[1,136,128]{2,1,0:T(8,128)S(1)} custom-call(f32[1,136,128]{2,1,0:T(8,128)S(1)} %collective-permute-done.1.refs_0_, f32[1,136,128]{2,1,0:T(8,128)S(1)} %collective-permute-done.2.refs_1_, f32[1,136,128]{2,1,0:T(8,128)S(1)} %collective-permute-done.4.refs_2_, f32[1,136,128]{2,1,0:T(8,128)S(1)} %collective-permute-done.5.refs_3_, ...), custom_call_target="tpu_custom_call" | custom-call | tf_op jit(solution)/shard_map/factor/pallas_call | solution.py:327
  41.6 3.2 %collective-permute-start.11 = (f32[1,136,128]{2,1,0:T(8,128)S(1)}, f32[1,136,128]{2,1,0:T(8,128)S(1)}, u32[]{:S(2)}, u32[]{:S(2)}) collective-permute-start(f32[1,136,128]{2,1,0:T(8,128)S(1)} %factor.1.refs_0_), channel_id=1, source_target_pairs={{0,8},{1,9},{2,10},{3,11},{4,12},{5,13},{6,14},{7,15},{8,0},{9,1},... | collective-permute-start | bytes 208904 | tf_op jit(solution)/shard_map/ppermute | solution.py:266
  46.3 1.6 %collective-permute-done.11.refs_1_ = f32[1,136,128]{2,1,0:T(8,128)S(1)} collective-permute-done((f32[1,136,128]{2,1,0:T(8,128)S(1)}, f32[1,136,128]{2,1,0:T(8,128)S(1)}, u32[]{:S(2)}, u32[]{:S(2)}) %collective-permute-start.11) | collective-permute-done | bytes 69664 | tf_op jit(solution)/shard_map/ppermute | solution.py:266
  49.2 1.2 %collective-permute-start.18 = (f32[1,136,128]{2,1,0:T(8,128)S(1)}, f32[1,136,128]{2,1,0:T(8,128)S(1)}, u32[]{:S(2)}, u32[]{:S(2)}) collective-permute-start(f32[1,136,128]{2,1,0:T(8,128)S(1)} %collective-permute-done.17.refs_2_), channel_id=1, source_target_pairs={{0,2},{1,3},{2,0},{3,1},{4,6},{5,7},{6,4},{7,5},{8,10},{9,11},{10,... | collective-permute-start | bytes 208904 | tf_op jit(solution)/shard_map/ppermute | solution.py:266
  50.8 1.4 %collective-permute-done.12.refs_3_ = f32[1,136,128]{2,1,0:T(8,128)S(1)} collective-permute-done((f32[1,136,128]{2,1,0:T(8,128)S(1)}, f32[1,136,128]{2,1,0:T(8,128)S(1)}, u32[]{:S(2)}, u32[]{:S(2)}) %collective-permute-start.12) | collective-permute-done | bytes 69664 | tf_op jit(solution)/shard_map/ppermute | solution.py:266
  52.2 0.9 %collective-permute-start.13 = (f32[1,136,128]{2,1,0:T(8,128)S(1)}, f32[1,136,128]{2,1,0:T(8,128)S(1)}, u32[]{:S(2)}, u32[]{:S(2)}) collective-permute-start(f32[1,136,128]{2,1,0:T(8,128)S(1)} %collective-permute-done.12.refs_3_), channel_id=1, source_target_pairs={{0,2},{1,3},{2,0},{3,1},{4,6},{5,7},{6,4},{7,5},{8,10},{9,11},{10,... | collective-permute-start | bytes 208904 | tf_op jit(solution)/shard_map/ppermute | solution.py:266
  53.0 1.1 %own.1 = f32[1,128,128]{2,1,0:T(8,128)} custom-call(bf16[4096,128]{1,0:T(8,128)(2,1)S(1)} %copy-done), custom_call_target="tpu_custom_call" | custom-call | tf_op jit(solution)/shard_map/own/pallas_call | solution.py:343
  55.2 1.3 %collective-permute-done.13.refs_3_ = f32[1,136,128]{2,1,0:T(8,128)S(1)} collective-permute-done((f32[1,136,128]{2,1,0:T(8,128)S(1)}, f32[1,136,128]{2,1,0:T(8,128)S(1)}, u32[]{:S(2)}, u32[]{:S(2)}) %collective-permute-start.13) | collective-permute-done | bytes 69664 | tf_op jit(solution)/shard_map/ppermute | solution.py:266
  57.1 1.3 %shard_map.93.refs_7_ = f32[144,256]{1,0:T(8,128)S(1)} custom-call(f32[1,136,128]{2,1,0:T(8,128)S(1)} %factor.1.refs_0_, f32[1,136,128]{2,1,0:T(8,128)S(1)} %collective-permute-done.11.refs_1_, f32[1,136,128]{2,1,0:T(8,128)S(1)} %collective-permute-done.17.refs_2_, f32[1,136,128]{2,1,0:T(8,128)S(1)} %collective-permute-done.12.refs_3_, ...), custom_call_target="tpu_custom_call" | custom-call | tf_op jit(solution)/shard_map/pallas_call | solution.py:357
  58.4 1.3 %shard_map.94.refs_1_ = f32[144,256]{1,0:T(8,128)S(1)} custom-call(f32[1,136,128]{2,1,0:T(8,128)S(1)} %collective-permute-done.15.refs_0_, f32[1,136,128]{2,1,0:T(8,128)S(1)} %collective-permute-done.16.refs_1_, f32[1,136,128]{2,1,0:T(8,128)S(1)} %collective-permute-done.18.refs_2_, f32[1,136,128]{2,1,0:T(8,128)S(1)} %collective-permute-done.13.refs_3_, ...), custom_call_target="tpu_custom_call" | custom-call | tf_op jit(solution)/shard_map/pallas_call | solution.py:357
  59.7 1.1 %eliminate.1 = (f32[1,128,128]{2,1,0:T(8,128)}, f32[1,128]{1,0:T(1,128)}) custom-call(f32[1,136,128]{2,1,0:T(8,128)S(1)} %collective-permute-done.14.refs_0_, f32[144,256]{1,0:T(8,128)S(1)} %shard_map.94.refs_1_, bf16[8,128,256]{2,1,0:T(8,128)(2,1)S(1)} %get-tuple-element.30.refs_8_.refs_2_, bf16[8,128,256]{2,1,0:T(8,128)(2,1)S(1)} %get-tuple-element.31.refs_9_.refs_3_, ...), custom_call_target="tpu_custom_call" | custom-call | tf_op jit(solution)/shard_map/eliminate/pallas_call | solution.py:365
  (52 shorter events, 6.8 us)
Async XLA Ops:
  4.7 11.2 %collective-permute-start = (f32[2,136,128]{2,1,0:T(8,128)S(1)}, f32[2,136,128]{2,1,0:T(8,128)S(1)}, u32[]{:S(2)}, u32[]{:S(2)}) collective-permute-start(f32[2,136,128]{2,1,0:T(8,128)S(1)} %get-tuple-element.21), channel_id=1, source_target_pairs={{0,1},{1,0},{2,3},{3,2},{4,5},{5,4},{6,7},{7,6},{8,9},{9,8},{10,11... | collective-permute-start | bytes 417800 | tf_op jit(solution)/shard_map/ppermute | solution.py:266
  8.5 13.7 %collective-permute-start.3 = (f32[2,136,128]{2,1,0:T(8,128)S(1)}, f32[2,136,128]{2,1,0:T(8,128)S(1)}, u32[]{:S(2)}, u32[]{:S(2)}) collective-permute-start(f32[2,136,128]{2,1,0:T(8,128)S(1)} %get-tuple-element.25), channel_id=1, source_target_pairs={{0,1},{1,0},{2,3},{3,2},{4,5},{5,4},{6,7},{7,6},{8,9},{9,8},{10,11... | collective-permute-start | bytes 417800 | tf_op jit(solution)/shard_map/ppermute | solution.py:266
  11.8 11.3 %collective-permute-start.6 = (f32[2,136,128]{2,1,0:T(8,128)S(1)}, f32[2,136,128]{2,1,0:T(8,128)S(1)}, u32[]{:S(2)}, u32[]{:S(2)}) collective-permute-start(f32[2,136,128]{2,1,0:T(8,128)S(1)} %get-tuple-element.27), channel_id=1, source_target_pairs={{0,1},{1,0},{2,3},{3,2},{4,5},{5,4},{6,7},{7,6},{8,9},{9,8},{10,11... | collective-permute-start | bytes 417800 | tf_op jit(solution)/shard_map/ppermute | solution.py:266
  15.8 9.3 %collective-permute-start.9 = (f32[2,136,128]{2,1,0:T(8,128)S(1)}, f32[2,136,128]{2,1,0:T(8,128)S(1)}, u32[]{:S(2)}, u32[]{:S(2)}) collective-permute-start(f32[2,136,128]{2,1,0:T(8,128)S(1)} %get-tuple-element.29), channel_id=1, source_target_pairs={{0,1},{1,0},{2,3},{3,2},{4,5},{5,4},{6,7},{7,6},{8,9},{9,8},{10,11... | collective-permute-start | bytes 417800 | tf_op jit(solution)/shard_map/ppermute | solution.py:266
  15.9 10.7 %collective-permute-start.1 = (f32[1,136,128]{2,1,0:T(8,128)S(1)}, f32[1,136,128]{2,1,0:T(8,128)S(1)}, u32[]{:S(2)}, u32[]{:S(2)}) collective-permute-start(f32[1,136,128]{2,1,0:T(8,128)S(1)} %get-tuple-element.41), channel_id=1, source_target_pairs={{0,12},{1,13},{2,14},{3,15},{4,8},{5,9},{6,10},{7,11},{8,4},{9,5},... | collective-permute-start | bytes 208904 | tf_op jit(solution)/shard_map/ppermute | solution.py:266
  21.0 8.1 %collective-permute-start.2 = (f32[1,136,128]{2,1,0:T(8,128)S(1)}, f32[1,136,128]{2,1,0:T(8,128)S(1)}, u32[]{:S(2)}, u32[]{:S(2)}) collective-permute-start(f32[1,136,128]{2,1,0:T(8,128)S(1)} %get-tuple-element.40), channel_id=1, source_target_pairs={{0,14},{1,15},{2,12},{3,13},{4,10},{5,11},{6,8},{7,9},{8,6},{9,7},... | collective-permute-start | bytes 208904 | tf_op jit(solution)/shard_map/ppermute | solution.py:266
  22.2 10.0 %collective-permute-start.4 = (f32[1,136,128]{2,1,0:T(8,128)S(1)}, f32[1,136,128]{2,1,0:T(8,128)S(1)}, u32[]{:S(2)}, u32[]{:S(2)}) collective-permute-start(f32[1,136,128]{2,1,0:T(8,128)S(1)} %get-tuple-element.39), channel_id=1, source_target_pairs={{0,8},{1,9},{2,10},{3,11},{4,12},{5,13},{6,14},{7,15},{8,0},{9,1},... | collective-permute-start | bytes 208904 | tf_op jit(solution)/shard_map/ppermute | solution.py:266
  23.1 11.0 %collective-permute-start.5 = (f32[1,136,128]{2,1,0:T(8,128)S(1)}, f32[1,136,128]{2,1,0:T(8,128)S(1)}, u32[]{:S(2)}, u32[]{:S(2)}) collective-permute-start(f32[1,136,128]{2,1,0:T(8,128)S(1)} %get-tuple-element.38), channel_id=1, source_target_pairs={{0,10},{1,11},{2,8},{3,9},{4,14},{5,15},{6,12},{7,13},{8,2},{9,3},... | collective-permute-start | bytes 208904 | tf_op jit(solution)/shard_map/ppermute | solution.py:266
  25.0 9.0 %collective-permute-start.7 = (f32[1,136,128]{2,1,0:T(8,128)S(1)}, f32[1,136,128]{2,1,0:T(8,128)S(1)}, u32[]{:S(2)}, u32[]{:S(2)}) collective-permute-start(f32[1,136,128]{2,1,0:T(8,128)S(1)} %get-tuple-element.37), channel_id=1, source_target_pairs={{0,4},{1,5},{2,6},{3,7},{4,0},{5,1},{6,2},{7,3},{8,12},{9,13},{10,... | collective-permute-start | bytes 208904 | tf_op jit(solution)/shard_map/ppermute | solution.py:266
  26.6 7.5 %collective-permute-start.8 = (f32[1,136,128]{2,1,0:T(8,128)S(1)}, f32[1,136,128]{2,1,0:T(8,128)S(1)}, u32[]{:S(2)}, u32[]{:S(2)}) collective-permute-start(f32[1,136,128]{2,1,0:T(8,128)S(1)} %get-tuple-element.36), channel_id=1, source_target_pairs={{0,6},{1,7},{2,4},{3,5},{4,2},{5,3},{6,0},{7,1},{8,14},{9,15},{10,... | collective-permute-start | bytes 208904 | tf_op jit(solution)/shard_map/ppermute | solution.py:266
  29.1 5.5 %collective-permute-start.10 = (f32[1,136,128]{2,1,0:T(8,128)S(1)}, f32[1,136,128]{2,1,0:T(8,128)S(1)}, u32[]{:S(2)}, u32[]{:S(2)}) collective-permute-start(f32[1,136,128]{2,1,0:T(8,128)S(1)} %get-tuple-element.42), channel_id=1, source_target_pairs={{0,2},{1,3},{2,0},{3,1},{4,6},{5,7},{6,4},{7,5},{8,10},{9,11},{10,... | collective-permute-start | bytes 208904 | tf_op jit(solution)/shard_map/ppermute | solution.py:266
  41.6 6.3 %collective-permute-start.11 = (f32[1,136,128]{2,1,0:T(8,128)S(1)}, f32[1,136,128]{2,1,0:T(8,128)S(1)}, u32[]{:S(2)}, u32[]{:S(2)}) collective-permute-start(f32[1,136,128]{2,1,0:T(8,128)S(1)} %factor.1.refs_0_), channel_id=1, source_target_pairs={{0,8},{1,9},{2,10},{3,11},{4,12},{5,13},{6,14},{7,15},{8,0},{9,1},... | collective-permute-start | bytes 208904 | tf_op jit(solution)/shard_map/ppermute | solution.py:266
  44.8 4.3 %collective-permute-start.17 = (f32[1,136,128]{2,1,0:T(8,128)S(1)}, f32[1,136,128]{2,1,0:T(8,128)S(1)}, u32[]{:S(2)}, u32[]{:S(2)}) collective-permute-start(f32[1,136,128]{2,1,0:T(8,128)S(1)} %factor.1.refs_0_), channel_id=1, source_target_pairs={{0,4},{1,5},{2,6},{3,7},{4,0},{5,1},{6,2},{7,3},{8,12},{9,13},{10,... | collective-permute-start | bytes 208904 | tf_op jit(solution)/shard_map/ppermute | solution.py:266
  45.6 4.7 %collective-permute-start.15 = (f32[1,136,128]{2,1,0:T(8,128)S(1)}, f32[1,136,128]{2,1,0:T(8,128)S(1)}, u32[]{:S(2)}, u32[]{:S(2)}) collective-permute-start(f32[1,136,128]{2,1,0:T(8,128)S(1)} %factor.1.refs_0_), channel_id=1, source_target_pairs={{0,2},{1,3},{2,0},{3,1},{4,6},{5,7},{6,4},{7,5},{8,10},{9,11},{10,... | collective-permute-start | bytes 208904 | tf_op jit(solution)/shard_map/ppermute | solution.py:266
  46.3 4.0 %collective-permute-start.22 = (f32[1,136,128]{2,1,0:T(8,128)S(1)}, f32[1,136,128]{2,1,0:T(8,128)S(1)}, u32[]{:S(2)}, u32[]{:S(2)}) collective-permute-start(f32[1,136,128]{2,1,0:T(8,128)S(1)} %factor.1.refs_0_), channel_id=1, source_target_pairs={{0,1},{1,0},{2,3},{3,2},{4,5},{5,4},{6,7},{7,6},{8,9},{9,8},{10,11... | collective-permute-start | bytes 208904 | tf_op jit(solution)/shard_map/ppermute | solution.py:266
  47.9 4.3 %collective-permute-start.12 = (f32[1,136,128]{2,1,0:T(8,128)S(1)}, f32[1,136,128]{2,1,0:T(8,128)S(1)}, u32[]{:S(2)}, u32[]{:S(2)}) collective-permute-start(f32[1,136,128]{2,1,0:T(8,128)S(1)} %collective-permute-done.11.refs_1_), channel_id=1, source_target_pairs={{0,4},{1,5},{2,6},{3,7},{4,0},{5,1},{6,2},{7,3},{8,12},{9,13},{10,... | collective-permute-start | bytes 208904 | tf_op jit(solution)/shard_map/ppermute | solution.py:266
  48.3 5.9 %collective-permute-start.16 = (f32[1,136,128]{2,1,0:T(8,128)S(1)}, f32[1,136,128]{2,1,0:T(8,128)S(1)}, u32[]{:S(2)}, u32[]{:S(2)}) collective-permute-start(f32[1,136,128]{2,1,0:T(8,128)S(1)} %collective-permute-done.11.refs_1_), channel_id=1, source_target_pairs={{0,2},{1,3},{2,0},{3,1},{4,6},{5,7},{6,4},{7,5},{8,10},{9,11},{10,... | collective-permute-start | bytes 208904 | tf_op jit(solution)/shard_map/ppermute | solution.py:266
  49.2 5.0 %collective-permute-start.18 = (f32[1,136,128]{2,1,0:T(8,128)S(1)}, f32[1,136,128]{2,1,0:T(8,128)S(1)}, u32[]{:S(2)}, u32[]{:S(2)}) collective-permute-start(f32[1,136,128]{2,1,0:T(8,128)S(1)} %collective-permute-done.17.refs_2_), channel_id=1, source_target_pairs={{0,2},{1,3},{2,0},{3,1},{4,6},{5,7},{6,4},{7,5},{8,10},{9,11},{10,... | collective-permute-start | bytes 208904 | tf_op jit(solution)/shard_map/ppermute | solution.py:266
  50.3 4.4 %collective-permute-start.23 = (f32[1,136,128]{2,1,0:T(8,128)S(1)}, f32[1,136,128]{2,1,0:T(8,128)S(1)}, u32[]{:S(2)}, u32[]{:S(2)}) collective-permute-start(f32[1,136,128]{2,1,0:T(8,128)S(1)} %collective-permute-done.11.refs_1_), channel_id=1, source_target_pairs={{0,1},{1,0},{2,3},{3,2},{4,5},{5,4},{6,7},{7,6},{8,9},{9,8},{10,11... | collective-permute-start | bytes 208904 | tf_op jit(solution)/shard_map/ppermute | solution.py:266
  50.3 4.4 %collective-permute-start.24 = (f32[1,136,128]{2,1,0:T(8,128)S(1)}, f32[1,136,128]{2,1,0:T(8,128)S(1)}, u32[]{:S(2)}, u32[]{:S(2)}) collective-permute-start(f32[1,136,128]{2,1,0:T(8,128)S(1)} %collective-permute-done.17.refs_2_), channel_id=1, source_target_pairs={{0,1},{1,0},{2,3},{3,2},{4,5},{5,4},{6,7},{7,6},{8,9},{9,8},{10,11... | collective-permute-start | bytes 208904 | tf_op jit(solution)/shard_map/ppermute | solution.py:266
  52.2 4.3 %collective-permute-start.13 = (f32[1,136,128]{2,1,0:T(8,128)S(1)}, f32[1,136,128]{2,1,0:T(8,128)S(1)}, u32[]{:S(2)}, u32[]{:S(2)}) collective-permute-start(f32[1,136,128]{2,1,0:T(8,128)S(1)} %collective-permute-done.12.refs_3_), channel_id=1, source_target_pairs={{0,2},{1,3},{2,0},{3,1},{4,6},{5,7},{6,4},{7,5},{8,10},{9,11},{10,... | collective-permute-start | bytes 208904 | tf_op jit(solution)/shard_map/ppermute | solution.py:266
  54.2 4.2 %collective-permute-start.19 = (f32[1,136,128]{2,1,0:T(8,128)S(1)}, f32[1,136,128]{2,1,0:T(8,128)S(1)}, u32[]{:S(2)}, u32[]{:S(2)}) collective-permute-start(f32[1,136,128]{2,1,0:T(8,128)S(1)} %collective-permute-done.15.refs_0_), channel_id=1, source_target_pairs={{0,1},{1,0},{2,3},{3,2},{4,5},{5,4},{6,7},{7,6},{8,9},{9,8},{10,11... | collective-permute-start | bytes 208904 | tf_op jit(solution)/shard_map/ppermute | solution.py:266
  54.7 3.7 %collective-permute-start.20 = (f32[1,136,128]{2,1,0:T(8,128)S(1)}, f32[1,136,128]{2,1,0:T(8,128)S(1)}, u32[]{:S(2)}, u32[]{:S(2)}) collective-permute-start(f32[1,136,128]{2,1,0:T(8,128)S(1)} %collective-permute-done.16.refs_1_), channel_id=1, source_target_pairs={{0,1},{1,0},{2,3},{3,2},{4,5},{5,4},{6,7},{7,6},{8,9},{9,8},{10,11... | collective-permute-start | bytes 208904 | tf_op jit(solution)/shard_map/ppermute | solution.py:266
  54.7 3.7 %collective-permute-start.21 = (f32[1,136,128]{2,1,0:T(8,128)S(1)}, f32[1,136,128]{2,1,0:T(8,128)S(1)}, u32[]{:S(2)}, u32[]{:S(2)}) collective-permute-start(f32[1,136,128]{2,1,0:T(8,128)S(1)} %collective-permute-done.18.refs_2_), channel_id=1, source_target_pairs={{0,1},{1,0},{2,3},{3,2},{4,5},{5,4},{6,7},{7,6},{8,9},{9,8},{10,11... | collective-permute-start | bytes 208904 | tf_op jit(solution)/shard_map/ppermute | solution.py:266
  (7 other events, 61.1 us)
